TPU v7x, 32 devices: a whole 2x2x4 slice. The times are simulated.
32 devices in a mesh: wide: 8 (over y, x, core), narrow: 4 (over z).
Axes of the slice: x: 2, y: 2, z: 4, core: 2. Of those that a mesh axis runs over, the one named last changes fastest.
Arguments:
- patches: bfloat16 [768, 50, 1024], P(('wide', 'narrow')), may hold values from -6 to 6
- keep_order: int32 [768, 50], P(('wide', 'narrow')), may hold values from 0 to 49, each once within a row
- keep_count: int32 [768], P(('wide', 'narrow')), may hold values from 25 to 50, as said below
- ln1_gain: bfloat16 [1024], P(('wide', 'narrow')), may hold values from 0.5 to 1.5
- ln1_bias: bfloat16 [1024], P(('wide', 'narrow')), may hold values from -1.796875 to 1.796875
- w_qkv: bfloat16 [1024, 3072], P(('wide', 'narrow')), may hold values from -0.1875 to 0.1875
- bias_q: bfloat16 [1024], P(('wide', 'narrow')), may hold values from -1.796875 to 1.796875
- bias_v: bfloat16 [1024], P(('wide', 'narrow')), may hold values from -1.796875 to 1.796875
- w_out: bfloat16 [1024, 1024], P(('wide', 'narrow')), may hold values from -0.5 to 0.5
- bias_out: bfloat16 [1024], P(('wide', 'narrow')), may hold values from -1.796875 to 1.796875
- ln2_gain: bfloat16 [1024], P(('wide', 'narrow')), may hold values from 0.5 to 1.5
- ln2_bias: bfloat16 [1024], P(('wide', 'narrow')), may hold values from -1.796875 to 1.796875
- w_up: bfloat16 [1024, 4096], P(('wide', 'narrow')), may hold values from -0.1875 to 0.1875
- bias_up: bfloat16 [4096], P(('wide', 'narrow')), may hold values from -1.796875 to 1.796875
- w_down: bfloat16 [4096, 1024], P(('wide', 'narrow')), may hold values from -0.125 to 0.125
- bias_down: bfloat16 [1024], P(('wide', 'narrow')), may hold values from -1.796875 to 1.796875
- cotangent: bfloat16 [768, 50, 1024], P(('wide', 'narrow')), may hold values from -6 to 6
Outputs:
- block_out: bfloat16 [768, 50, 1024], P(('wide', 'narrow'))
- grad_patches: bfloat16 [768, 50, 1024], P(('wide', 'narrow'))
- grad_ln1_gain: float32 [1024], P(('wide', 'narrow'))
- grad_ln1_bias: float32 [1024], P(('wide', 'narrow'))
- grad_w_qkv: float32 [1024, 3072], P(('wide', 'narrow'))
- grad_bias_q: float32 [1024], P(('wide', 'narrow'))
- grad_bias_v: float32 [1024], P(('wide', 'narrow'))
- grad_w_out: float32 [1024, 1024], P(('wide', 'narrow'))
- grad_bias_out: float32 [1024], P(('wide', 'narrow'))
- grad_ln2_gain: float32 [1024], P(('wide', 'narrow'))
- grad_ln2_bias: float32 [1024], P(('wide', 'narrow'))
- grad_w_up: float32 [1024, 4096], P(('wide', 'narrow'))
- grad_bias_up: float32 [4096], P(('wide', 'narrow'))
- grad_w_down: float32 [4096, 1024], P(('wide', 'narrow'))
- grad_bias_down: float32 [1024], P(('wide', 'narrow'))
Inputs may be any that keep to these rules, and one draw needn't show every extreme that they name: `keep_order`: each row lists every slot of its image once; the first keep_count of them are the kept slots. `keep_count`: in every draw some image keeps all 50 slots and some image keeps 50 // 2.
All inputs are finite; a program needn't handle non-finite values.
Results may differ from a plain program's by a relative error of at most 0.012.
Values may be sent and summed in bfloat16 or wider, within the bound.
No kernel may reach another device: no remote copies, remote signals or barrier semaphores. Data moves between devices by JAX's collectives and lax.ppermute only.
A program may use at most 256 MiB of HBM per device.

v0:
```python
import jax
import jax.numpy as jnp
from jax import lax
from jax.sharding import PartitionSpec as P

HEADS = 16


eps_norm = 1e-06


def layer_norm(row_data, gain_vec, offset):
    center = row_data - jnp.mean(row_data, axis=-1, keepdims=True)
    spread = jnp.mean(center * center, axis=-1, keepdims=True)
    return center * lax.rsqrt(spread + eps_norm) * gain_vec + offset


def gelu_exact(values_in):
    return jax.nn.gelu(values_in, approximate=False)


def kept_slots(keep_order, keep_count):
    slot_ids = lax.iota(jnp.int32, keep_order.shape[-1])
    listed = keep_order[:, :, None] == slot_ids[None, None, :]
    within = slot_ids[None, :] < keep_count[:, None]
    return jnp.any(jnp.logical_and(listed, within[:, :, None]), axis=1)


def rows_product(left_side, right_side):
    return lax.dot_general(
        left_side, right_side, (((0,), (0,)), ((), ())), preferred_element_type=jnp.float32
    )


def back_product(left_side, right_side):
    return lax.dot_general(
        left_side, right_side, (((1,), (1,)), ((), ())), preferred_element_type=jnp.float32
    )


def column_sum(low_rows):
    return jnp.sum(low_rows.astype(jnp.float32), axis=0)


def local(
    patches,
    keep_order,
    keep_count,
    ln1_gain,
    ln1_bias,
    w_qkv,
    bias_q,
    bias_v,
    w_out,
    bias_out,
    ln2_gain,
    ln2_bias,
    w_up,
    bias_up,
    w_down,
    bias_down,
    cotangent,
):
    image_count, slot_count, model_width = patches.shape
    row_count = image_count * slot_count
    head_size = model_width // HEADS
    scale_factor = head_size ** (-0.5)
    head_shape = (image_count, slot_count, HEADS, head_size)
    keep_mask = kept_slots(keep_order, keep_count)
    keep_rows = keep_mask.reshape(row_count, 1)
    key_live = keep_mask[:, None, None, :]
    gathered = (
        lax.all_gather(ln1_gain, ("wide", "narrow"), axis=0, tiled=True),
        lax.all_gather(ln1_bias, ("wide", "narrow"), axis=0, tiled=True),
        lax.all_gather(w_qkv, ("wide", "narrow"), axis=0, tiled=True),
        lax.all_gather(bias_q, ("wide", "narrow"), axis=0, tiled=True),
        lax.all_gather(bias_v, ("wide", "narrow"), axis=0, tiled=True),
        lax.all_gather(w_out, ("wide", "narrow"), axis=0, tiled=True),
        lax.all_gather(bias_out, ("wide", "narrow"), axis=0, tiled=True),
        lax.all_gather(ln2_gain, ("wide", "narrow"), axis=0, tiled=True),
        lax.all_gather(ln2_bias, ("wide", "narrow"), axis=0, tiled=True),
        lax.all_gather(w_up, ("wide", "narrow"), axis=0, tiled=True),
        lax.all_gather(bias_up, ("wide", "narrow"), axis=0, tiled=True),
        lax.all_gather(w_down, ("wide", "narrow"), axis=0, tiled=True),
        lax.all_gather(bias_down, ("wide", "narrow"), axis=0, tiled=True),
    )
    (
        gain_one,
        offset_one,
        qkv_full,
        q_bias_full,
        v_bias_full,
        out_full,
        out_bias_full,
        gain_two,
        offset_two,
        up_full,
        up_bias_full,
        down_full,
        down_bias_full,
    ) = gathered
    row_data = patches.astype(jnp.float32).reshape(row_count, model_width)
    normed_one = layer_norm(
        row_data, gain_one.astype(jnp.float32), offset_one.astype(jnp.float32)
    ).astype(jnp.bfloat16)
    projected = jnp.dot(normed_one, qkv_full, preferred_element_type=jnp.float32)
    queries = (
        (projected[:, :model_width] + q_bias_full.astype(jnp.float32))
        .astype(jnp.bfloat16)
        .reshape(head_shape)
    )
    key_rows = projected[:, model_width : 2 * model_width].astype(jnp.bfloat16).reshape(head_shape)
    value_rows = (
        (projected[:, 2 * model_width :] + v_bias_full.astype(jnp.float32))
        .astype(jnp.bfloat16)
        .reshape(head_shape)
    )
    scores = (
        jnp.einsum("bqhe,bkhe->bhqk", queries, key_rows, preferred_element_type=jnp.float32)
        * scale_factor
    )
    masked = jnp.where(key_live, scores, -jnp.inf)
    row_peak = jnp.max(masked, axis=-1, keepdims=True)
    exp_terms = jnp.exp(masked - row_peak)
    exp_total = jnp.sum(exp_terms, axis=-1, keepdims=True)
    probs_low = (exp_terms / exp_total).astype(jnp.bfloat16)
    log_total = row_peak + jnp.log(exp_total)
    attn_mixed = (
        jnp.einsum("bhqk,bkhe->bqhe", probs_low, value_rows, preferred_element_type=jnp.float32)
        .reshape(row_count, model_width)
        .astype(jnp.bfloat16)
    )
    residual = (
        row_data
        + jnp.dot(attn_mixed, out_full, preferred_element_type=jnp.float32)
        + out_bias_full.astype(jnp.float32)
    )
    normed_two = layer_norm(
        residual, gain_two.astype(jnp.float32), offset_two.astype(jnp.float32)
    ).astype(jnp.bfloat16)
    hidden = jnp.dot(normed_two, up_full, preferred_element_type=jnp.float32) + up_bias_full.astype(
        jnp.float32
    )
    activated = gelu_exact(hidden).astype(jnp.bfloat16)
    summed_out = (
        residual
        + jnp.dot(activated, down_full, preferred_element_type=jnp.float32)
        + down_bias_full.astype(jnp.float32)
    )
    block_out = (
        jnp.where(keep_rows, summed_out, 0.0)
        .astype(jnp.bfloat16)
        .reshape(image_count, slot_count, model_width)
    )
    back_set = (
        lax.all_gather(ln1_gain, ("wide", "narrow"), axis=0, tiled=True),
        lax.all_gather(ln1_bias, ("wide", "narrow"), axis=0, tiled=True),
        lax.all_gather(w_qkv, ("wide", "narrow"), axis=0, tiled=True),
        lax.all_gather(bias_q, ("wide", "narrow"), axis=0, tiled=True),
        lax.all_gather(bias_v, ("wide", "narrow"), axis=0, tiled=True),
        lax.all_gather(w_out, ("wide", "narrow"), axis=0, tiled=True),
        lax.all_gather(bias_out, ("wide", "narrow"), axis=0, tiled=True),
        lax.all_gather(ln2_gain, ("wide", "narrow"), axis=0, tiled=True),
        lax.all_gather(ln2_bias, ("wide", "narrow"), axis=0, tiled=True),
        lax.all_gather(w_up, ("wide", "narrow"), axis=0, tiled=True),
        lax.all_gather(bias_up, ("wide", "narrow"), axis=0, tiled=True),
        lax.all_gather(w_down, ("wide", "narrow"), axis=0, tiled=True),
        lax.all_gather(bias_down, ("wide", "narrow"), axis=0, tiled=True),
    )
    (
        gain_one_back,
        offset_one_back,
        qkv_back,
        q_bias_back,
        v_bias_back,
        out_back,
        out_bias_back,
        gain_two_back,
        offset_two_back,
        up_back,
        up_bias_back,
        down_back,
        down_bias_back,
    ) = back_set
    grad_top = jnp.where(
        keep_rows, cotangent.astype(jnp.float32).reshape(row_count, model_width), 0.0
    )
    grad_top_low = grad_top.astype(jnp.bfloat16)
    grad_bias_down = column_sum(grad_top_low)
    grad_w_down = rows_product(activated, grad_top_low)
    grad_activated = back_product(grad_top_low, down_back)
    gelu_pull = jax.vjp(gelu_exact, hidden)[1]
    grad_hidden = gelu_pull(grad_activated)[0].astype(jnp.bfloat16)
    grad_bias_up = column_sum(grad_hidden)
    grad_w_up = rows_product(normed_two, grad_hidden)
    grad_normed_two = back_product(grad_hidden, up_back)
    norm_two_pull = jax.vjp(
        layer_norm, residual, gain_two_back.astype(jnp.float32), offset_two_back.astype(jnp.float32)
    )[1]
    grad_resid_norm, grad_ln2_gain, grad_ln2_bias = norm_two_pull(grad_normed_two)
    grad_residual = grad_top + grad_resid_norm
    grad_branch = grad_residual.astype(jnp.bfloat16)
    grad_bias_out = column_sum(grad_branch)
    grad_w_out = rows_product(attn_mixed, grad_branch)
    grad_mixed = back_product(grad_branch, out_back).astype(jnp.bfloat16).reshape(head_shape)
    scores_again = (
        jnp.einsum("bqhe,bkhe->bhqk", queries, key_rows, preferred_element_type=jnp.float32)
        * scale_factor
    )
    probs_again = jnp.exp(jnp.where(key_live, scores_again, -jnp.inf) - log_total)
    probs_again_low = probs_again.astype(jnp.bfloat16)
    grad_values = jnp.einsum(
        "bhqk,bqhe->bkhe", probs_again_low, grad_mixed, preferred_element_type=jnp.float32
    ).astype(jnp.bfloat16)
    grad_probs = jnp.einsum(
        "bqhe,bkhe->bhqk", grad_mixed, value_rows, preferred_element_type=jnp.float32
    )
    grad_scores = (
        probs_again * (grad_probs - jnp.sum(probs_again * grad_probs, axis=-1, keepdims=True))
    ).astype(jnp.bfloat16)
    grad_queries = (
        (
            jnp.einsum("bhqk,bkhe->bqhe", grad_scores, key_rows, preferred_element_type=jnp.float32)
            * scale_factor
        )
        .astype(jnp.bfloat16)
        .reshape(row_count, model_width)
    )
    grad_keys = (
        (
            jnp.einsum("bhqk,bqhe->bkhe", grad_scores, queries, preferred_element_type=jnp.float32)
            * scale_factor
        )
        .astype(jnp.bfloat16)
        .reshape(row_count, model_width)
    )
    grad_values_flat = grad_values.reshape(row_count, model_width)
    grad_projected = jnp.concatenate([grad_queries, grad_keys, grad_values_flat], axis=1)
    grad_bias_q = column_sum(grad_queries)
    grad_bias_v = column_sum(grad_values_flat)
    grad_w_qkv = rows_product(normed_one, grad_projected)
    grad_normed_one = back_product(grad_projected, qkv_back)
    norm_one_pull = jax.vjp(
        layer_norm, row_data, gain_one_back.astype(jnp.float32), offset_one_back.astype(jnp.float32)
    )[1]
    grad_rows_norm, grad_ln1_gain, grad_ln1_bias = norm_one_pull(grad_normed_one)
    grad_patches = (
        (grad_residual + grad_rows_norm)
        .astype(jnp.bfloat16)
        .reshape(image_count, slot_count, model_width)
    )
    owned = (
        lax.psum_scatter(grad_ln1_gain, ("wide", "narrow"), scatter_dimension=0, tiled=True),
        lax.psum_scatter(grad_ln1_bias, ("wide", "narrow"), scatter_dimension=0, tiled=True),
        lax.psum_scatter(grad_w_qkv, ("wide", "narrow"), scatter_dimension=0, tiled=True),
        lax.psum_scatter(grad_bias_q, ("wide", "narrow"), scatter_dimension=0, tiled=True),
        lax.psum_scatter(grad_bias_v, ("wide", "narrow"), scatter_dimension=0, tiled=True),
        lax.psum_scatter(grad_w_out, ("wide", "narrow"), scatter_dimension=0, tiled=True),
        lax.psum_scatter(grad_bias_out, ("wide", "narrow"), scatter_dimension=0, tiled=True),
        lax.psum_scatter(grad_ln2_gain, ("wide", "narrow"), scatter_dimension=0, tiled=True),
        lax.psum_scatter(grad_ln2_bias, ("wide", "narrow"), scatter_dimension=0, tiled=True),
        lax.psum_scatter(grad_w_up, ("wide", "narrow"), scatter_dimension=0, tiled=True),
        lax.psum_scatter(grad_bias_up, ("wide", "narrow"), scatter_dimension=0, tiled=True),
        lax.psum_scatter(grad_w_down, ("wide", "narrow"), scatter_dimension=0, tiled=True),
        lax.psum_scatter(grad_bias_down, ("wide", "narrow"), scatter_dimension=0, tiled=True),
    )
    return (
        block_out,
        grad_patches,
        owned[0],
        owned[1],
        owned[2],
        owned[3],
        owned[4],
        owned[5],
        owned[6],
        owned[7],
        owned[8],
        owned[9],
        owned[10],
        owned[11],
        owned[12],
    )


def solution(mesh):
    in_specs = (
        P(("wide", "narrow"), None, None),
        P(("wide", "narrow"), None),
        P(("wide", "narrow")),
        P(("wide", "narrow")),
        P(("wide", "narrow")),
        P(("wide", "narrow"), None),
        P(("wide", "narrow")),
        P(("wide", "narrow")),
        P(("wide", "narrow"), None),
        P(("wide", "narrow")),
        P(("wide", "narrow")),
        P(("wide", "narrow")),
        P(("wide", "narrow"), None),
        P(("wide", "narrow")),
        P(("wide", "narrow"), None),
        P(("wide", "narrow")),
        P(("wide", "narrow"), None, None),
    )
    out_specs = (
        P(("wide", "narrow"), None, None),
        P(("wide", "narrow"), None, None),
        P(("wide", "narrow")),
        P(("wide", "narrow")),
        P(("wide", "narrow"), None),
        P(("wide", "narrow")),
        P(("wide", "narrow")),
        P(("wide", "narrow"), None),
        P(("wide", "narrow")),
        P(("wide", "narrow")),
        P(("wide", "narrow")),
        P(("wide", "narrow"), None),
        P(("wide", "narrow")),
        P(("wide", "narrow"), None),
        P(("wide", "narrow")),
    )
    return jax.shard_map(local, mesh=mesh, in_specs=in_specs, out_specs=out_specs, check_vma=False)
```

profile of v0, /device:TPU:0, one launch (start us, length us, event | category | flops | bytes accessed | tf_op | source)
XLA Modules:
  0.0 1401.4 jit_solution(6089318124187900606)
XLA Ops:
  20.1 42.8 %all-reduce.18 = (bf16[1024]{0:T(1024)(128)(2,1)S(1)}, bf16[1024]{0:T(1024)(128)(2,1)S(1)}, bf16[1024]{0:T(1024)(128)(2,1)S(1)}, bf16[1024]{0:T(1024)(128)(2,1)S...) all-reduce(bf16[1024]{0:T(1024)(128)(2,1)S(1)} %dynamic-update-slic, ...), channel_id=1, replica_groups=mesh['wide'=8,'narrow'=4] {'wide','narrow'}, use_global_device_ids=true, to_apply=%add.1 | all-reduce | flops 8192 | bytes 32768
  63.0 66.8 %all-gather = bf16[32,1,128]{2,1,0:T(2,128)(2,1)S(1)} all-gather(bf16[1,1,128]{2,1,0:T(2,128)(2,1)S(1)} %bitcast.44), channel_id=1, replica_groups=mesh['wide'=8,'narrow'=4] {'wide','narrow'}, dimensions={0}, use_global_device_ids=true | all-gather | bytes 8448 | tf_op jit(solution)/shard_map/all_gather | solution.py:83
  149.5 12.0 fusion.52
  166.3 7.5 reshape.197
  173.8 7.5 reshape.199
  186.3 12.0 fusion.28
  198.3 8.3 fusion.6
  208.1 7.3 convert_bitcast_fusion.1
  221.1 6.5 convert_element_type.137
  227.6 6.9 fusion.57
  238.1 58.7 %multiply_convert_fusion = (bf16[1200,4096]{1,0:T(8,128)(2,1)}, f32[1200,4096]{1,0:T(8,128)}, f32[1200,4096]{1,0:T(8,128)}) fusion(f32[4096]{0:T(1024)S(1)} %bitcast.43, bf16[1024,4096]{1,0:T(8,128)(2,1)} %all-gather.10.cloned.1.call-done, f32[1200,1024]{1,0:T(8,128)} %copy-done.4, f32[1024]{0:T(1024)S(1)} %convert_element_type.140, ...), kind=kOutput, calls=%fused_computation.4 | convolution fusion | flops 10396876800 | bytes 62489984 | tf_op jit(solution)/shard_map/dot_general | solution.py:141
  298.6 28.0 %convert_reduce_fusion = (f32[4096]{0:T(1024)}, bf16[1200,4096]{1,0:T(8,128)(2,1)}) fusion(f32[1200,4096]{1,0:T(8,128)} %get-tuple-element.120, f32[1200,4096]{1,0:T(8,128)} %get-tuple-element.127, bf16[4096,1024]{1,0:T(8,128)(2,1)} %all-gather.12.cloned.1.call-done, f32[1200,1024]{1,0:T(8,128)} %reshape.201, pred[1200]{0:T(1024)(128)(4,1)S(1)} %copy-done.28), kind=kOutput, calls=%fused_computation.2 | convolution fusion | flops 10146197504 | bytes 62473392 | tf_op jit(solution)/shard_map/dot_general | solution.py:36
  326.7 20.0 %multiply_reduce_fusion.1 = (f32[1024]{0:T(1024)}, f32[1200]{0:T(1024)S(1)}, f32[1024]{0:T(1024)}, f32[1200,1024]{1,0:T(8,128)S(1)}) fusion(f32[1200,1024]{1,0:T(8,128)} %copy-done.4, f32[1200]{0:T(1024)S(1)} %fusion.41, f32[1200]{0:T(1024)S(1)} %broadcast_multiply_fusion.1, f32[1024]{0:T(1024)S(1)} %convert_element_type.139, ...), kind=kOutput, calls=%fused_computation.59 | convolution fusion | flops 10076156928 | bytes 28076096 | tf_op jit(solution)/shard_map/dot_general | solution.py:36
  357.8 6.4 convolution_convert_fusion
  364.2 7.7 reshape.202
  371.9 16.2 %multiply_reduce_fusion = (f32[24,16,50]{2,1,0:T(8,128)}, f32[24,16,50,50]{2,3,1,0:T(8,128)}) fusion(f32[24,16,50]{2,1,0:T(8,128)S(1)} %copy-done.10, f32[24,16,50,50]{2,3,1,0:T(8,128)} %get-tuple-element.124, pred[24,50]{1,0:T(8,128)(4,1)S(1)} %copy-done.14, bf16[24,50,16,64]{3,2,1,0:T(8,128)(2,1)} %reshape.197, bf16[24,50,16,64]{3,2,1,0:T(8,128)(2,1)} %reshape.202), kind=kOutput, calls=%fused_computation.24 | convolution fusion | flops 127660800 | bytes 12750000 | tf_op jit(solution)/shard_map/bqhe,bkhe->bhqk/dot_general | solution.py:215
  388.1 9.2 multiply_convert_fusion.3
  397.3 9.5 fusion.11
  412.5 6.7 reshape.204
  419.2 10.1 convert_reduce_fusion.2
  434.7 7.6 reshape.203
  442.4 12.6 convert_reduce_fusion.1
  460.5 7.9 reshape.205
  474.2 11.5 fusion.51
  486.3 19.0 %fusion.53 = f32[1024,4096]{1,0:T(8,128)} fusion(bf16[1200,4096]{1,0:T(8,128)(2,1)} %get-tuple-element.137, f32[1200,1024]{1,0:T(8,128)} %copy-done.4, f32[1024]{0:T(1024)S(1)} %copy-done.32, f32[1024]{0:T(1024)S(1)} %convert_element_type.139, f32[1200]{0:T(1024)S(1)} %fusion.41, f32[1200]{0:T(1024)S(1)} %broadcast_multiply_fusion.1), kind=kOutput, calls=%fused_computation.104 | convolution fusion | flops 10072473600 | bytes 31540608 | tf_op jit(solution)/shard_map/dot_general | solution.py:30
  505.4 19.1 %fusion.49 = f32[4096,1024]{1,0:T(8,128)} fusion(bf16[1200,4096]{1,0:T(8,128)(2,1)} %get-tuple-element.119, f32[1200,1024]{1,0:T(8,128)} %reshape.201, pred[1200]{0:T(1024)(128)(4,1)S(1)} %copy-done.28), kind=kOutput, calls=%fused_computation.100 | convolution fusion | flops 10067558400 | bytes 31524016 | tf_op jit(solution)/shard_map/dot_general | solution.py:30
  526.9 18.0 %select_convert_fusion.1 = bf16[1200,1024]{1,0:T(8,128)(2,1)} fusion(f32[1200,1024]{1,0:T(8,128)} %copy-done.4, bf16[1200,4096]{1,0:T(8,128)(2,1)} %get-tuple-element.119, bf16[4096,1024]{1,0:T(8,128)(2,1)} %all-gather.12.cloned.1.call-done, f32[1024]{0:T(1024)S(1)} %convert_element_type.144, pred[1200]{0:T(1024)(128)(4,1)S(1)} %copy-done.28), kind=kOutput, calls=%fused_computation.66 | convolution fusion | flops 10071244800 | bytes 25597104 | tf_op jit(solution)/shard_map/dot_general | solution.py:147
  550.7 16.6 %multiply_reduce_fusion.2 = (f32[1024]{0:T(1024)S(1)}, f32[1200]{0:T(1024)S(1)}, f32[1024]{0:T(1024)S(1)}, f32[1200,1024]{1,0:T(8,128)}) fusion(f32[1200,1024]{1,0:T(8,128)} %reshape.196, f32[1200]{0:T(1024)S(1)} %copy-done.22, f32[1200]{0:T(1024)S(1)} %copy-done.20, f32[1024]{0:T(1024)S(1)} %copy-done.26, bf16[1200,3072]{1,0:T(8,128)(2,1)} %copy-done.11, ...), kind=kOutput, calls=%fused_computation.61 | convolution fusion | flops 7559574528 | bytes 23521344 | tf_op jit(solution)/shard_map/dot_general | solution.py:36
  567.3 42.7 %all-reduce.17 = (f32[1024]{0:T(1024)S(1)}, f32[1024]{0:T(1024)S(1)}, f32[1024]{0:T(1024)S(1)}, f32[1024]{0:T(1024)S(1)}, f32[1024]{0:T(1024)S(1)}, /*index=5*/f...) all-reduce(f32[1024]{0:T(1024)S(1)} %get-tuple-element.92, ...), channel_id=2, replica_groups=mesh['wide'=8,'narrow'=4] {'wide','narrow'}, use_global_device_ids=true, to_apply=%region_13.14.clone | all-reduce | flops 12288 | bytes 98304
  630.1 37.1 %reduce-scatter.5.cloned.1.call-done = f32[32,3072]{1,0:T(8,128)} async-done(((f32[1024,3072]{1,0:T(8,128)}), f32[32,3072]{1,0:T(8,128)}) %reduce-scatter.5.cloned.1.call-update) | async-done | bytes 393232 | tf_op jit(solution)/shard_map/reduce_scatter | solution.py:255
  667.2 362.4 %reduce-scatter.9.cloned.1.call-done = f32[32,4096]{1,0:T(8,128)} async-done(((f32[1024,4096]{1,0:T(8,128)}), f32[32,4096]{1,0:T(8,128)}) %reduce-scatter.9.cloned.1.call-update) | async-done | bytes 524304 | tf_op jit(solution)/shard_map/reduce_scatter | solution.py:262
  1029.6 364.8 %reduce-scatter.11.cloned.1.call-done = f32[128,1024]{1,0:T(8,128)} async-done(((f32[4096,1024]{1,0:T(8,128)}), f32[128,1024]{1,0:T(8,128)}) %reduce-scatter.11.cloned.1.call-update) | async-done | bytes 524304 | tf_op jit(solution)/shard_map/reduce_scatter | solution.py:264
  (215 shorter events, 116.8 us)
Async XLA Ops:
  7.2 142.3 %all-gather.6.cloned.1.call-start = ((), (), s32[]{:S(2)}) async-start(), calls=%async_computation.4 | async-start | bytes 6488064 | tf_op jit(solution)/shard_map/all_gather | solution.py:75
  7.9 219.7 %all-gather.8.cloned.1.call-start = ((), (), s32[]{:S(2)}) async-start(), calls=%async_computation.5 | async-start | bytes 2162688 | tf_op jit(solution)/shard_map/all_gather | solution.py:78
  8.7 229.3 %all-gather.10.cloned.1.call-start = ((), (), s32[]{:S(2)}) async-start(), calls=%async_computation.6 | async-start | bytes 8650752 | tf_op jit(solution)/shard_map/all_gather | solution.py:82
  9.5 53.5 %copy-start.37 = (s32[24]{0:T(128)S(1)}, s32[24]{0:T(128)}, u32[]{:S(2)}) copy-start(s32[24]{0:T(128)} %param.19) | copy-start | bytes 292
  9.5 53.5 %copy-start.36 = (bf16[128]{0:T(256)(128)(2,1)S(1)}, bf16[128]{0:T(256)(128)(2,1)}, u32[]{:S(2)}) copy-start(bf16[128]{0:T(256)(128)(2,1)} %param.30) | copy-start | bytes 772
  9.5 120.3 %copy-start.27 = (s32[24,50]{1,0:T(8,128)S(1)}, s32[24,50]{1,0:T(8,128)}, u32[]{:S(2)}) copy-start(s32[24,50]{1,0:T(8,128)} %param.18) | copy-start | bytes 14404
  9.5 121.6 %copy-start.1 = (bf16[24,50,1024]{2,0,1:T(8,128)(2,1)S(1)}, bf16[24,50,1024]{2,0,1:T(8,128)(2,1)}, u32[]{:S(2)}) copy-start(bf16[24,50,1024]{2,0,1:T(8,128)(2,1)} %param.17) | copy-start | bytes 7372804
  9.5 289.1 %all-gather.12.cloned.1.call-start = ((), (), s32[]{:S(2)}) async-start(), calls=%async_computation.7 | async-start | bytes 8650752 | tf_op jit(solution)/shard_map/all_gather | solution.py:84
  10.1 620.0 %reduce-scatter.7.cloned.1.call-start = ((), (), s32[]{:S(2)}) async-start(), calls=%async_computation.9 | async-start | bytes 4325376 | tf_op jit(solution)/shard_map/reduce_scatter | solution.py:258
  12.5 136.9 %copy-start.19 = (f32[1200]{0:T(1024)}, f32[1200]{0:T(1024)S(1)}, u32[]{:S(2)}) copy-start(f32[1200]{0:T(1024)S(1)} %div.51) | copy-start | bytes 14404
  62.9 86.6 %copy-start.33 = (f32[1024]{0:T(1024)}, f32[1024]{0:T(1024)S(1)}, u32[]{:S(2)}) copy-start(f32[1024]{0:T(1024)S(1)} %convert_element_type.128) | copy-start | bytes 12292
  62.9 86.6 %copy-start.25 = (f32[1024]{0:T(1024)}, f32[1024]{0:T(1024)S(1)}, u32[]{:S(2)}) copy-start(f32[1024]{0:T(1024)S(1)} %convert_element_type.127) | copy-start | bytes 12292
  62.9 175.1 %copy-start.31 = (f32[1024]{0:T(1024)}, f32[1024]{0:T(1024)S(1)}, u32[]{:S(2)}) copy-start(f32[1024]{0:T(1024)S(1)} %convert_element_type.140) | copy-start | bytes 12292
  130.4 77.6 %copy-start.13 = (pred[24,50]{1,0:T(8,128)(4,1)}, pred[24,50]{1,0:T(8,128)(4,1)S(1)}, u32[]{:S(2)}) copy-start(pred[24,50]{1,0:T(8,128)(4,1)S(1)} %fusion.40) | copy-start | bytes 3604
  132.2 17.3 %copy-start.21 = (f32[1200]{0:T(1024)}, f32[1200]{0:T(1024)S(1)}, u32[]{:S(2)}) copy-start(f32[1200]{0:T(1024)S(1)} %rsqrt.22) | copy-start | bytes 14404
  181.3 26.7 %slice-start.3 = ((s8[4915200]{0:T(1024)(128)(4,1)}), s8[720896]{0:T(1024)(128)(4,1)S(1)}, s32[]{:S(2)}) async-start(s8[4915200]{0:T(1024)(128)(4,1)} %bitcast.39), calls=%async_computation.15 | async-start | bytes 1441792
  186.3 21.8 %slice-start.4 = ((s8[4915200]{0:T(1024)(128)(4,1)}), s8[4194304]{0:T(1024)(128)(4,1)S(1)}, s32[]{:S(2)}) async-start(s8[4915200]{0:T(1024)(128)(4,1)} %bitcast.39), calls=%async_computation.16 | async-start | bytes 8388608
  238.0 60.6 %copy-start.28 = (pred[1200]{0:T(1024)(128)(4,1)S(1)}, pred[1200]{0:T(1024)(128)(4,1)}, u32[]{:S(2)}) copy-start(pred[1200]{0:T(1024)(128)(4,1)} %broadcast_in_dim.46) | copy-start | bytes 3604
  326.7 20.0 %copy-start.16 = (f32[1200]{0:T(1024)S(1)}, f32[1200]{0:T(1024)}, u32[]{:S(2)}) copy-start(f32[1200]{0:T(1024)} %copy-done.15) | copy-start | bytes 14404
  326.7 20.1 %copy-start.5 = (f32[1200,1024]{1,0:T(8,128)S(1)}, f32[1200,1024]{1,0:T(8,128)}, u32[]{:S(2)}) copy-start(f32[1200,1024]{1,0:T(8,128)} %copy-done.4) | copy-start | bytes 14745604
  357.7 309.5 %reduce-scatter.5.cloned.1.call-start = ((), (), s32[]{:S(2)}) async-start(), calls=%async_computation.8 | async-start | bytes 12976128 | tf_op jit(solution)/shard_map/reduce_scatter | solution.py:255
  364.2 23.9 %slice-start = ((s8[11010048]{0:T(1024)(128)(4,1)}), s8[2621440]{0:T(1024)(128)(4,1)S(1)}, s32[]{:S(2)}) async-start(s8[11010048]{0:T(1024)(128)(4,1)} %bitcast.37), calls=%async_computation.12 | async-start | bytes 5242880
  371.9 16.3 %slice-start.1 = ((s8[11010048]{0:T(1024)(128)(4,1)}), s8[4194304]{0:T(1024)(128)(4,1)S(1)}, s32[]{:S(2)}) async-start(s8[11010048]{0:T(1024)(128)(4,1)} %bitcast.37), calls=%async_computation.13 | async-start | bytes 8388608
  371.9 16.3 %slice-start.2 = ((s8[11010048]{0:T(1024)(128)(4,1)}), s8[4194304]{0:T(1024)(128)(4,1)S(1)}, s32[]{:S(2)}) async-start(s8[11010048]{0:T(1024)(128)(4,1)} %bitcast.37), calls=%async_computation.14 | async-start | bytes 8388608
  460.5 13.6 slice-start.5
  485.7 543.9 %reduce-scatter.9.cloned.1.call-start = ((), (), s32[]{:S(2)}) async-start(), calls=%async_computation.10 | async-start | bytes 17301504 | tf_op jit(solution)/shard_map/reduce_scatter | solution.py:262
  505.4 889.0 %reduce-scatter.11.cloned.1.call-start = ((), (), s32[]{:S(2)}) async-start(), calls=%async_computation.11 | async-start | bytes 17301504 | tf_op jit(solution)/shard_map/reduce_scatter | solution.py:264
  550.7 16.6 %copy-start.23 = (f32[4096]{0:T(1024)S(1)}, f32[4096]{0:T(1024)}, u32[]{:S(2)}) copy-start(f32[4096]{0:T(1024)} %get-tuple-element.136) | copy-start | bytes 49156
  550.7 16.6 %copy-start.24 = (f32[1024]{0:T(1024)S(1)}, f32[1024]{0:T(1024)}, u32[]{:S(2)}) copy-start(f32[1024]{0:T(1024)} %get-tuple-element.113) | copy-start | bytes 12292
  550.7 16.6 %copy-start.29 = (f32[1024]{0:T(1024)S(1)}, f32[1024]{0:T(1024)}, u32[]{:S(2)}) copy-start(f32[1024]{0:T(1024)} %get-tuple-element.90) | copy-start | bytes 12292
  550.7 16.6 %copy-start.30 = (f32[1024]{0:T(1024)S(1)}, f32[1024]{0:T(1024)}, u32[]{:S(2)}) copy-start(f32[1024]{0:T(1024)} %get-tuple-element.94) | copy-start | bytes 12292
  550.7 64.0 %copy-start.18 = (f32[1200]{0:T(1024)S(1)}, f32[1200]{0:T(1024)}, u32[]{:S(2)}) copy-start(f32[1200]{0:T(1024)} %copy-done.17) | copy-start | bytes 14404
  (30 other events, 170.6 us)
Sparse Core Ops, SparseCore 0:
  10.9 72.5 all-gather.5
  86.4 54.7 all-gather.7
  144.2 75.9 all-gather.9
  222.9 75.6 all-gather.11
  357.9 147.5 reduce-scatter.6
  511.9 155.2 reduce-scatter.4
  670.1 359.4 reduce-scatter.8
  1032.5 361.9 reduce-scatter.10
where the time goes:
time: 1410 us; the launch traced here: 1400 us
  waiting for transfers between devices  769 us (55%)
  matrix products  289 us (20%)
  blocking collectives  152 us (11%)
  local copies, waits for them, and re-layouts  137 us (10%)
  other arithmetic  39.6 us (3%)
  between operations  15.1 us (1%)
    reduce_scatter x1, waiting for transfers between devices, local(): lax.psum_scatter(grad_w_down, ('wide', 'narrow'), scatter_dimension=0, ti...  365 us
    reduce_scatter x1, waiting for transfers between devices, local(): lax.psum_scatter(grad_w_up, ('wide', 'narrow'), scatter_dimension=0, tile...  362 us
    unnamed x2, blocking collectives  85.5 us
    dot_general x4, matrix products, back_product(): lax.dot_general(left_side, right_side, (((1,), (1,)), ((), ())), preferre...  71.1 us
    all_gather x1, blocking collectives, local(): lax.all_gather(bias_up, ('wide', 'narrow'), axis=0, tiled=True)  66.8 us
    dot_general x1, matrix products, local(): jnp.dot(normed_two, up_full, preferred_element_type=jnp.float32)  58.7 us
    dot_general x4, matrix products, rows_product(): lax.dot_general(left_side, right_side, (((0,), (0,)), ((), ())), preferre...  54.1 us
    reduce_scatter x1, waiting for transfers between devices, local(): lax.psum_scatter(grad_w_qkv, ('wide', 'narrow'), scatter_dimension=0, til...  37.1 us
  transfers between devices with their start and end apart: 8, of which 4 were waited for; matrix products, arithmetic and copies ran while one was open for 28% of the time, Pallas kernels for 0%

commit v1 on v0

v1 whole, which is shorter than its diff:
```python
import functools

import jax
import jax.numpy as jnp
import numpy as np
from jax import lax
from jax.experimental import pallas as pl
from jax.experimental.pallas import tpu as pltpu
from jax.sharding import PartitionSpec as P

HEADS = 16
EPS = 1e-06
AXES = ("wide", "narrow")
BF = jnp.bfloat16
F32 = jnp.float32
NEG = -1e30
VMEM_LIMIT = 62 << 20
IMG_BLOCK = 8


class Layout:
    def __init__(self, mesh):
        self.wide = mesh.shape["wide"]
        self.narrow = mesh.shape["narrow"]
        self.count = self.wide * self.narrow
        self.chip_bits = (self.wide // 2).bit_length() - 1
        self.line_bits = self.narrow.bit_length() - 1

    def bit_of(self, core, level):
        return level if core == 0 else self.chip_bits - 1 - level

    def flip(self, core, piece):
        total = 0
        for level in range(self.chip_bits):
            if piece >> level & 1:
                total ^= 1 << self.bit_of(core, level)
        return total

    def swap_line(self, bit):
        return [(d, d ^ (1 << bit)) for d in range(self.count)]

    def swap_core(self):
        return [(d, d ^ self.narrow) for d in range(self.count)]

    def swap_chip(self, level):
        pairs = []
        for d in range(self.count):
            place, line = divmod(d, self.narrow)
            chip, core = divmod(place, 2)
            other = chip ^ (1 << self.bit_of(core, level))
            pairs.append((d, (other * 2 + core) * self.narrow + line))
        return pairs

    def swap_chip_bit(self, bit):
        return [(d, d ^ (2 * self.narrow << bit)) for d in range(self.count)]

    def table(self):
        place = lax.axis_index("wide")
        chip, core = place // 2, place % 2
        half = 1 << self.chip_bits
        even = np.array([self.flip(0, q) for q in range(half)], np.int32)
        odd = np.array([self.flip(1, q) for q in range(half)], np.int32)
        mine = jnp.where(core == 0, even, odd)
        other = jnp.where(core == 0, odd, even)
        return jnp.concatenate(
            [(chip ^ mine) * 2 + core, (chip ^ other) * 2 + (1 - core)]
        ).astype(jnp.int32)


def move(x, pairs):
    return lax.ppermute(x, AXES, pairs)


def in_order(bit, mine, theirs):
    return jnp.where(
        bit == 0, jnp.concatenate([mine, theirs], 0), jnp.concatenate([theirs, mine], 0)
    )


def gather_line(lay, shard):
    line = lax.axis_index("narrow")
    for b in range(lay.line_bits):
        shard = in_order((line >> b) & 1, shard, move(shard, lay.swap_line(b)))
    return shard


def gather_pieces(lay, shard):
    pieces = [gather_line(lay, shard)]
    for level in range(lay.chip_bits):
        pieces = pieces + [move(p, lay.swap_chip(level)) for p in pieces]
    return pieces + [move(p, lay.swap_core()) for p in pieces]


def gather_small(lay, shard):
    whole = gather_line(lay, shard)
    place = lax.axis_index("wide")
    whole = in_order(place & 1, whole, move(whole, lay.swap_core()))
    for b in range(lay.chip_bits):
        whole = in_order((place >> (b + 1)) & 1, whole, move(whole, lay.swap_chip_bit(b)))
    return whole


def plus(a, b, dtype=BF):
    return (a.astype(F32) + b.astype(F32)).astype(dtype)


def halve(x, bit, pairs, dtype):
    size = x.shape[0] // 2
    give = lax.dynamic_slice_in_dim(x, (1 - bit) * size, size, 0)
    keep = lax.dynamic_slice_in_dim(x, bit * size, size, 0)
    return plus(keep, move(give, pairs), dtype)


def scatter_line(lay, x, dtype):
    line = lax.axis_index("narrow")
    for b in reversed(range(lay.line_bits)):
        x = halve(x, (line >> b) & 1, lay.swap_line(b), F32 if b == 0 else dtype)
    return x


def scatter_pieces(lay, give, keep):
    x = plus(keep, move(give, lay.swap_core()))
    for level in reversed(range(lay.chip_bits)):
        size = x.shape[0] // 2
        x = plus(x[:size], move(x[size:], lay.swap_chip(level)))
    return scatter_line(lay, x, BF)


def scatter_small(lay, x):
    place = lax.axis_index("wide")
    for b in reversed(range(lay.chip_bits)):
        x = halve(x, (place >> (b + 1)) & 1, lay.swap_chip_bit(b), F32)
    x = halve(x, place & 1, lay.swap_core(), F32)
    return scatter_line(lay, x, F32)


def dot_nn(a, b):
    return jnp.dot(a, b, preferred_element_type=F32)


def dot_nt(a, b):
    return lax.dot_general(a, b, (((1,), (1,)), ((), ())), preferred_element_type=F32)


def dot_tn(a, b):
    return lax.dot_general(a, b, (((0,), (0,)), ((), ())), preferred_element_type=F32)


def normalize(r):
    center = r - jnp.mean(r, axis=-1, keepdims=True)
    spread = jnp.mean(center * center, axis=-1, keepdims=True)
    rinv = lax.rsqrt(spread + EPS)
    return center * rinv, rinv


def norm_back(up, gain, n, rinv):
    u = up * gain
    return rinv * (
        u - jnp.mean(u, axis=-1, keepdims=True) - n * jnp.mean(u * n, axis=-1, keepdims=True)
    )


def col_sum(x):
    return jnp.sum(x, axis=0, keepdims=True)


def call(body, outs, grid, in_specs, out_specs, scratch, flops, nbytes, name, trans=0):
    return pl.pallas_call(
        body,
        out_shape=outs,
        grid_spec=pltpu.PrefetchScalarGridSpec(
            num_scalar_prefetch=1,
            grid=grid,
            in_specs=in_specs,
            out_specs=out_specs,
            scratch_shapes=scratch,
        ),
        compiler_params=pltpu.CompilerParams(vmem_limit_bytes=VMEM_LIMIT),
        cost_estimate=pl.CostEstimate(flops=flops, bytes_accessed=nbytes, transcendentals=trans),
        name=name,
    )


def full(shape):
    zeros = (0,) * len(shape)
    return pl.BlockSpec(shape, lambda *_: zeros)


def anywhere(count):
    return [pl.BlockSpec(memory_space=pl.ANY)] * count


def sds(shape, dtype):
    return jax.ShapeDtypeStruct(shape, dtype)


def fill_tile(tab, pieces, tile):
    size = pieces[0].shape[0]
    for p, piece in enumerate(pieces):
        tile[pl.ds(pl.multiple_of(tab[p] * size, size), size), :] = piece[...]


def load_copies(tab, pieces, store, sem):
    size = pieces[0].shape[0]
    return [
        pltpu.make_async_copy(
            piece,
            store.at[pl.ds(pl.multiple_of(tab[p] * size, size), size)],
            sem.at[p],
        )
        for p, piece in enumerate(pieces)
    ]


def row_chunk(rows):
    for size in (240, 200, 160, 80, 48, 16):
        if rows % size == 0:
            return size
    return rows


def qkv_product(tab, x, gain, bias, bias_qkv, pieces):
    rows, width = x.shape
    cols = pieces[0].shape[1]
    tn = 512
    count = len(pieces)
    chunk = row_chunk(rows)

    def body(tab_ref, x_ref, g_ref, b_ref, c_ref, *rest):
        piece_refs, (n_ref, o_ref, tile) = rest[:count], rest[count:]

        @pl.when(pl.program_id(0) == 0)
        def _():
            @pl.loop(0, rows // chunk)
            def _(i):
                at = pl.ds(pl.multiple_of(i * chunk, chunk), chunk)
                n, _unused = normalize(x_ref[at, :].astype(F32))
                n_ref[at, :] = (n * g_ref[...] + b_ref[...]).astype(BF)

        fill_tile(tab_ref, piece_refs, tile)
        o_ref[...] = (dot_nn(n_ref[...], tile[...]) + c_ref[...]).astype(BF)

    size = pieces[0].shape[0]
    return call(
        body,
        (sds((rows, width), BF), sds((rows, cols), BF)),
        (cols // tn,),
        [full((rows, width)), full((1, width)), full((1, width))]
        + [pl.BlockSpec((1, tn), lambda j, t: (0, j))]
        + [pl.BlockSpec((size, tn), lambda j, t: (0, j))] * count,
        (full((rows, width)), pl.BlockSpec((rows, tn), lambda j, t: (0, j))),
        [pltpu.VMEM((width, tn), BF)],
        2 * rows * width * cols,
        2 * (2 * rows * width + rows * cols + width * cols),
        "qkv_product",
    )(tab, x, gain, bias, bias_qkv, *pieces)


def two_heads(x, lane):
    return jnp.concatenate([jnp.where(lane < 64, x, 0.0), jnp.where(lane < 64, 0.0, x)], 0).astype(
        BF
    )


def half_max(s, low):
    a = jnp.max(jnp.where(low, s, NEG), axis=-1, keepdims=True)
    b = jnp.max(jnp.where(low, NEG, s), axis=-1, keepdims=True)
    return jnp.where(low, a, b)


def half_sum(s, low):
    a = jnp.sum(jnp.where(low, s, 0.0), axis=-1, keepdims=True)
    b = jnp.sum(jnp.where(low, 0.0, s), axis=-1, keepdims=True)
    return jnp.where(low, a, b)


def softmax_pair(q, kk, key_bias, low, scale):
    s = dot_nt(q, kk) * scale + key_bias
    e = jnp.exp(s - half_max(s, low))
    return e / half_sum(e, low)


def attention(tab, qkv, key_bias, slots):
    rows, three = qkv.shape
    width = three // 3
    pairs = width // 128
    blk = IMG_BLOCK * slots
    pad = -(-slots // 8) * 8
    scale = float(64**-0.5)

    def body(tab_ref, q_ref, k_ref, v_ref, kb_ref, o_ref, qf, kf, vf, of):
        qf[0:blk, :] = q_ref[...].astype(F32)
        kf[0:blk, :] = k_ref[...].astype(F32)
        vf[0:blk, :] = v_ref[...].astype(F32)
        kf[blk : blk + 16, :] = jnp.zeros((16, 128), F32)
        vf[blk : blk + 16, :] = jnp.zeros((16, 128), F32)
        qf[blk : blk + 16, :] = jnp.zeros((16, 128), F32)
        lane = lax.broadcasted_iota(jnp.int32, (64, 128), 1)
        low = lax.broadcasted_iota(jnp.int32, (pad, 128), 1) < 64
        for b in range(IMG_BLOCK):
            at = slots * b
            kk = two_heads(kf[at : at + 64, :], lane)
            vv = two_heads(vf[at : at + 64, :], lane)
            q = qf[at : at + pad, :].astype(BF)
            p = softmax_pair(q, kk, kb_ref[b], low, scale)
            of[at : at + pad, :] = dot_nn(p.astype(BF), vv)
        o_ref[...] = of[0:blk, :].astype(BF)

    return call(
        body,
        sds((rows, width), BF),
        (pairs, rows // blk),
        [
            pl.BlockSpec((blk, 128), lambda h, i, t: (i, h)),
            pl.BlockSpec((blk, 128), lambda h, i, t: (i, h + pairs)),
            pl.BlockSpec((blk, 128), lambda h, i, t: (i, h + 2 * pairs)),
            pl.BlockSpec((IMG_BLOCK, 1, 128), lambda h, i, t: (i, 0, 0)),
        ],
        pl.BlockSpec((blk, 128), lambda h, i, t: (i, h)),
        [pltpu.VMEM((blk + 16, 128), F32)] * 4,
        8 * rows * 128 * width * 2,
        2 * 4 * rows * width,
        "attention",
    )(tab, qkv, qkv, qkv, key_bias)


def attention_back(tab, qkv, key_bias, grad_mixed, slots):
    rows, three = qkv.shape
    width = three // 3
    pairs = width // 128
    blk = IMG_BLOCK * slots
    pad = -(-slots // 8) * 8
    scale = float(64**-0.5)

    def body(tab_ref, q_ref, k_ref, v_ref, kb_ref, g_ref, o_ref, s_ref, qf, kf, vf, gf, *outs):
        dqf, dkf, dvf = outs
        for ref, src in ((qf, q_ref), (kf, k_ref), (vf, v_ref), (gf, g_ref)):
            ref[0:blk, :] = src[...].astype(F32)
            ref[blk : blk + 16, :] = jnp.zeros((16, 128), F32)
        lane = lax.broadcasted_iota(jnp.int32, (64, 128), 1)
        low = lax.broadcasted_iota(jnp.int32, (pad, 128), 1) < 64
        real = lax.broadcasted_iota(jnp.int32, (pad, 128), 0) < slots
        for b in range(IMG_BLOCK):
            at = slots * b
            kk = two_heads(kf[at : at + 64, :], lane)
            vv = two_heads(vf[at : at + 64, :], lane)
            q = jnp.where(real, qf[at : at + pad, :], 0.0).astype(BF)
            g = jnp.where(real, gf[at : at + pad, :], 0.0).astype(BF)
            p = softmax_pair(q, kk, kb_ref[b], low, scale)
            dp = dot_nt(g, vv)
            ds = (p * (dp - half_sum(p * dp, low))).astype(BF)
            dqf[at : at + pad, :] = dot_nn(ds, kk) * scale
            dk = dot_tn(ds, q) * scale
            dv = dot_tn(p.astype(BF), g)
            dkf[at : at + pad, :] = jnp.where(low, dk[0:pad], dk[64 : 64 + pad])
            dvf[at : at + pad, :] = jnp.where(low, dv[0:pad], dv[64 : 64 + pad])
        @pl.when(pl.program_id(1) == 0)
        def _():
            s_ref[...] = jnp.zeros_like(s_ref)

        for at, ref in enumerate((dqf, dkf, dvf)):
            rounded = ref[0:blk, :].astype(BF)
            o_ref[at] = rounded
            s_ref[at : at + 1, :] += col_sum(rounded.astype(F32))

    spec = pl.BlockSpec((blk, 128), lambda h, i, t: (i, h))
    return call(
        body,
        (sds((3, rows, width), BF), sds((8, width), F32)),
        (pairs, rows // blk),
        [
            spec,
            pl.BlockSpec((blk, 128), lambda h, i, t: (i, h + pairs)),
            pl.BlockSpec((blk, 128), lambda h, i, t: (i, h + 2 * pairs)),
            pl.BlockSpec((IMG_BLOCK, 1, 128), lambda h, i, t: (i, 0, 0)),
            spec,
        ],
        (
            pl.BlockSpec((3, blk, 128), lambda h, i, t: (0, i, h)),
            pl.BlockSpec((8, 128), lambda h, i, t: (0, h)),
        ),
        [pltpu.VMEM((blk + 16, 128), F32)] * 7,
        20 * rows * 128 * width * 2,
        2 * 7 * rows * width,
        "attention_back",
    )(tab, qkv, qkv, qkv, key_bias, grad_mixed)


def out_product(tab, mixed, x, bias_out, gain, bias, pieces, slots):
    rows, width = mixed.shape
    blk = IMG_BLOCK * slots
    count = len(pieces)

    def body(tab_ref, m_ref, x_ref, c_ref, g_ref, b_ref, *rest):
        piece_refs, (r_ref, n_ref, store, sem) = rest[:count], rest[count:]

        @pl.when(pl.program_id(0) == 0)
        def _():
            copies = load_copies(tab_ref, piece_refs, store, sem)
            for c in copies:
                c.start()
            for c in copies:
                c.wait()

        r = x_ref[...].astype(F32) + dot_nn(m_ref[...], store[...]) + c_ref[...]
        r_ref[...] = r
        n, _unused = normalize(r)
        n_ref[...] = (n * g_ref[...] + b_ref[...]).astype(BF)

    spec = pl.BlockSpec((blk, width), lambda i, t: (i, 0))
    return call(
        body,
        (sds((rows, width), F32), sds((rows, width), BF)),
        (rows // blk,),
        [spec, spec] + [full((1, width))] * 3 + anywhere(count),
        (spec, spec),
        [pltpu.VMEM((width, width), BF), pltpu.SemaphoreType.DMA((count,))],
        2 * rows * width * width,
        10 * rows * width + 2 * width * width,
        "out_product",
    )(tab, mixed, x, bias_out, gain, bias, *pieces)


def up_product(tab, n2, bias_up, pieces):
    rows, width = n2.shape
    hid = pieces[0].shape[1]
    count = len(pieces)
    tn = hid // count
    size = pieces[0].shape[0]

    def body(tab_ref, n_ref, c_ref, *rest):
        piece_refs, (a_ref, d_ref, tile) = rest[:count], rest[count:]
        fill_tile(tab_ref, piece_refs, tile)
        u = dot_nn(n_ref[...], tile[...]) + c_ref[...]
        phi = 0.5 + 0.5 * lax.erf(u * np.float32(0.5**0.5))
        a_ref[...] = (u * phi).astype(BF)
        slope = phi + u * jnp.exp(-0.5 * u * u) * np.float32((2 * np.pi) ** -0.5)
        d_ref[...] = slope.astype(BF)

    spec = pl.BlockSpec((rows, tn), lambda p, t: (0, p))
    return call(
        body,
        (sds((rows, hid), BF), sds((rows, hid), BF)),
        (count,),
        [full((rows, width)), pl.BlockSpec((1, tn), lambda p, t: (0, t[p]))]
        + [pl.BlockSpec((size, tn), lambda p, t: (0, t[p]))] * count,
        (spec, spec),
        [pltpu.VMEM((width, tn), BF)],
        2 * rows * width * hid + 30 * rows * hid,
        2 * (rows * width + 2 * rows * hid + width * hid),
        "up_product",
        2 * rows * hid,
    )(tab, n2, bias_up, *pieces)


def down_product(tab, act, residual, bias_down, keep, pieces, images, slots):
    rows, hid = act.shape
    size, width = pieces[0].shape
    blk = IMG_BLOCK * slots
    count = len(pieces)

    def body(tab_ref, a_ref, r_ref, c_ref, k_ref, *rest):
        piece_refs, (o_ref, store, sem) = rest[:count], rest[count:]

        @pl.when(pl.program_id(0) == 0)
        def _():
            copies = [
                pltpu.make_async_copy(ref, store.at[pl.ds(p * size, size)], sem.at[p])
                for p, ref in enumerate(piece_refs)
            ]
            for c in copies:
                c.start()
            for c in copies:
                c.wait()

        y = r_ref[...] + dot_nn(a_ref[...], store[...]) + c_ref[...]
        y = jnp.where(k_ref[...] > 0.0, y, 0.0)
        for b in range(IMG_BLOCK):
            o_ref[b] = y[slots * b : slots * (b + 1)].astype(BF)

    return call(
        body,
        sds((images, slots, width), BF),
        (rows // blk,),
        [
            pl.BlockSpec((blk, hid), lambda i, t: (i, 0)),
            pl.BlockSpec((blk, width), lambda i, t: (i, 0)),
            full((1, width)),
            pl.BlockSpec((blk, 1), lambda i, t: (i, 0)),
        ]
        + anywhere(count),
        pl.BlockSpec((IMG_BLOCK, slots, width), lambda i, t: (i, 0, 0)),
        [pltpu.VMEM((hid, width), BF), pltpu.SemaphoreType.DMA((count,))],
        2 * rows * width * hid,
        2 * (rows * hid + 3 * rows * width + width * hid),
        "down_product",
    )(tab, act, residual, bias_down, keep, *pieces)


def hidden_back(tab, top, slope, pieces):
    rows, width = top.shape
    hid = slope.shape[1]
    count = len(pieces)
    tn = hid // count

    def body(tab_ref, t_ref, d_ref, *rest):
        piece_refs, (o_ref, s_ref, store, sem) = rest[:count], rest[count:]
        p = pl.program_id(0)
        copies = [
            pltpu.make_async_copy(ref, store.at[at], sem.at[at])
            for at, ref in enumerate(piece_refs)
        ]

        @pl.when(p == 0)
        def _():
            for c in copies:
                c.start()

        pltpu.make_async_copy(store.at[p], store.at[p], sem.at[p]).wait()
        g = (dot_nt(t_ref[...], store[p]) * d_ref[...].astype(F32)).astype(BF)
        o_ref[...] = g
        s_ref[...] = col_sum(g.astype(F32))

    spec = pl.BlockSpec((rows, tn), lambda p, t: (0, p))
    return call(
        body,
        (sds((rows, hid), BF), sds((1, hid), F32)),
        (count,),
        [full((rows, width)), spec] + anywhere(count),
        (spec, pl.BlockSpec((1, tn), lambda p, t: (0, t[p]))),
        [pltpu.VMEM((count, tn, width), BF), pltpu.SemaphoreType.DMA((count,))],
        2 * rows * width * hid,
        2 * (rows * width + 2 * rows * hid + width * hid),
        "hidden_back",
    )(tab, top, slope, *pieces)


def up_back(tab, grad_hidden, residual, top, gain, pieces, out_pieces):
    rows, hid = grad_hidden.shape
    width = residual.shape[1]
    count = len(pieces)
    tn = hid // count
    size = pieces[0].shape[0]
    chunk = row_chunk(rows)

    def body(tab_ref, h_ref, r_ref, t_ref, g_ref, *rest):
        piece_refs, out_refs = rest[:count], rest[count : 2 * count]
        gr_ref, gb_ref, gm_ref, s_ref, tile, acc, store, sem = rest[2 * count :]
        p = pl.program_id(0)
        copies = load_copies(tab_ref, out_refs, store, sem)

        @pl.when(p == 0)
        def _():
            for c in copies:
                c.start()

        fill_tile(tab_ref, piece_refs, tile)
        part = dot_nt(h_ref[...], tile[...])

        @pl.when(p == 0)
        def _():
            acc[...] = part

        @pl.when(p > 0)
        def _():
            acc[...] += part

        @pl.when(p == count - 1)
        def _():
            for c in copies:
                c.wait()
            s_ref[...] = jnp.zeros_like(s_ref)

            @pl.loop(0, rows // chunk)
            def _(i):
                at = pl.ds(pl.multiple_of(i * chunk, chunk), chunk)
                n, rinv = normalize(r_ref[at, :])
                up = acc[at, :]
                grad = t_ref[at, :].astype(F32) + norm_back(up, g_ref[...], n, rinv)
                branch = grad.astype(BF)
                gr_ref[at, :] = grad
                gb_ref[at, :] = branch
                gm_ref[at, :] = dot_nt(branch, store[...]).astype(BF)
                s_ref[0:1, :] += col_sum(up * n)
                s_ref[1:2, :] += col_sum(up)
                s_ref[2:3, :] += col_sum(branch.astype(F32))
                s_ref[3:4, :] += col_sum(t_ref[at, :].astype(F32))

    whole = full((rows, width))
    return call(
        body,
        (
            sds((rows, width), F32),
            sds((rows, width), BF),
            sds((rows, width), BF),
            sds((8, width), F32),
        ),
        (count,),
        [pl.BlockSpec((rows, tn), lambda p, t: (0, p)), whole, whole, full((1, width))]
        + [pl.BlockSpec((size, tn), lambda p, t: (0, t[p]))] * count
        + anywhere(count),
        (whole, whole, whole, full((8, width))),
        [
            pltpu.VMEM((width, tn), BF),
            pltpu.VMEM((rows, width), F32),
            pltpu.VMEM((width, width), BF),
            pltpu.SemaphoreType.DMA((count,)),
        ],
        2 * rows * width * (hid + width),
        2 * (rows * hid + 8 * rows * width + width * hid),
        "up_back",
    )(tab, grad_hidden, residual, top, gain, *pieces, *out_pieces)


def qkv_back(tab, grads, x, grad_residual, gain, pieces, images, slots):
    _three, rows, width = grads.shape
    blk = IMG_BLOCK * slots
    count = len(pieces)

    def body(tab_ref, d_ref, x_ref, r_ref, g_ref, *rest):
        piece_refs, (o_ref, s_ref, store, sem) = rest[:count], rest[count:]

        @pl.when(pl.program_id(0) == 0)
        def _():
            copies = load_copies(tab_ref, piece_refs, store, sem)
            for c in copies:
                c.start()
            s_ref[...] = jnp.zeros_like(s_ref)
            for c in copies:
                c.wait()

        up = dot_nt(d_ref[0], store[:, 0:width])
        up += dot_nt(d_ref[1], store[:, width : 2 * width])
        up += dot_nt(d_ref[2], store[:, 2 * width :])
        n, rinv = normalize(x_ref[...].astype(F32))
        y = r_ref[...] + norm_back(up, g_ref[...], n, rinv)
        s_ref[0:1, :] += col_sum(up * n)
        s_ref[1:2, :] += col_sum(up)
        for b in range(IMG_BLOCK):
            o_ref[b] = y[slots * b : slots * (b + 1)].astype(BF)

    spec = pl.BlockSpec((blk, width), lambda i, t: (i, 0))
    return call(
        body,
        (sds((images, slots, width), BF), sds((8, width), F32)),
        (rows // blk,),
        [pl.BlockSpec((3, blk, width), lambda i, t: (0, i, 0)), spec, spec, full((1, width))]
        + anywhere(count),
        (pl.BlockSpec((IMG_BLOCK, slots, width), lambda i, t: (i, 0, 0)), full((8, width))),
        [pltpu.VMEM((width, 3 * width), BF), pltpu.SemaphoreType.DMA((count,))],
        6 * rows * width * width,
        2 * (3 * rows * width + 4 * rows * width + 3 * width * width),
        "qkv_back",
    )(tab, grads, x, grad_residual, gain, *pieces)


def weight_grad(order, x, g, pieces_of, name, places=None):
    parts, rows, width = g.shape
    count = order.shape[0]
    size = x.shape[1] // pieces_of

    def body(tab_ref, *rest):
        x_refs, (g_ref, o_ref, xs) = rest[:count], rest[count:]

        @pl.when(pl.program_id(0) == 0)
        def _():
            for p in range(count):
                xs[:, size * p : size * (p + 1)] = x_refs[p][...]

        o_ref[...] = dot_tn(xs[...], g_ref[0]).astype(BF)

    tn = width if places is None else width // places.shape[0]
    per = width // tn
    if places is None:
        table = order
        put = pl.BlockSpec((count * size, tn), lambda j, t: (0, j))
    else:
        table = jnp.concatenate([order, places])
        put = pl.BlockSpec((count * size, tn), lambda j, t: (0, t[count + j]))

    def column(p):
        return lambda j, t: (0, t[p])

    return call(
        body,
        sds((count * size, parts * width), BF),
        (parts * per,),
        [pl.BlockSpec((rows, size), column(p)) for p in range(count)]
        + [pl.BlockSpec((1, rows, tn), lambda j, t: (j // per, 0, j % per))],
        put,
        [pltpu.VMEM((rows, count * size), BF)],
        2 * rows * count * size * parts * width,
        2 * (rows * count * size + parts * rows * width + count * size * parts * width),
        name,
    )(table, *([x] * count), g)


def down_grad(order, act, top, pieces_of, name):
    rows, hid = act.shape
    width = top.shape[1]
    count = order.shape[0]
    size = hid // pieces_of

    def body(tab_ref, a_ref, t_ref, o_ref):
        o_ref[...] = dot_tn(a_ref[...], t_ref[...]).astype(BF)

    return call(
        body,
        sds((count * size, width), BF),
        (count,),
        [pl.BlockSpec((rows, size), lambda p, t: (0, t[p])), full((rows, width))],
        pl.BlockSpec((size, width), lambda p, t: (p, 0)),
        [],
        2 * rows * count * size * width,
        2 * (rows * count * size + rows * width + count * size * width),
        name,
    )(order, act, top)


def kept_slots(keep_order, keep_count):
    slot_ids = lax.iota(jnp.int32, keep_order.shape[-1])
    listed = keep_order[:, :, None] == slot_ids[None, None, :]
    within = slot_ids[None, :] < keep_count[:, None]
    return jnp.any(jnp.logical_and(listed, within[:, :, None]), axis=1)


def local(lay, *args):
    (
        patches,
        keep_order,
        keep_count,
        ln1_gain,
        ln1_bias,
        w_qkv,
        bias_q,
        bias_v,
        w_out,
        bias_out,
        ln2_gain,
        ln2_bias,
        w_up,
        bias_up,
        w_down,
        bias_down,
        cotangent,
    ) = args
    images, slots, width = patches.shape
    rows = images * slots
    ndev = lay.count
    own = width // ndev
    own_up = bias_up.shape[0]
    hid = own_up * ndev

    tab = lay.table()
    groups = lay.wide
    half = groups // 2

    small = jnp.concatenate(
        [ln1_gain, ln1_bias, bias_q, bias_v, bias_out, ln2_gain, ln2_bias, bias_down, bias_up]
    )[None, :]
    vec = gather_small(lay, small).astype(F32)
    eight = vec[:, : 8 * own].reshape(ndev, 8, own).transpose(1, 0, 2).reshape(8, 1, width)
    gain_one, offset_one, vec_q, vec_v, vec_out, gain_two, offset_two, vec_down = eight
    vec_up = vec[:, 8 * own :].reshape(1, hid)

    qkv_pieces = gather_pieces(lay, w_qkv)
    out_pieces = gather_pieces(lay, w_out)
    up_pieces = gather_pieces(lay, w_up)
    down_pieces = gather_pieces(lay, w_down)

    keep_mask = kept_slots(keep_order, keep_count)
    keep_rows = keep_mask.reshape(rows, 1)
    keep_f = keep_rows.astype(F32)
    pad_keys = jnp.pad(jnp.where(keep_mask, 0.0, NEG), ((0, 0), (0, 64 - slots)), constant_values=NEG)
    key_bias = jnp.concatenate([pad_keys, pad_keys], 1).reshape(images, 1, 128)
    x = patches.reshape(rows, width)
    top = jnp.where(keep_rows, cotangent.reshape(rows, width), jnp.zeros((), BF))

    vec_qkv = jnp.concatenate([vec_q, jnp.zeros_like(vec_q), vec_v], axis=1)
    normed_one, qkv = qkv_product(tab, x, gain_one, offset_one, vec_qkv, qkv_pieces)
    mixed = attention(tab, qkv, key_bias, slots)
    residual, normed_two = out_product(
        tab, mixed, x, vec_out, gain_two, offset_two, out_pieces, slots
    )
    act, slope = up_product(tab, normed_two, vec_up, up_pieces)
    block_out = down_product(
        tab, act, residual, vec_down, keep_f, down_pieces, images, slots
    )

    straight = jnp.arange(groups, dtype=jnp.int32)
    give_down = down_grad(straight[half:], act, top, groups, "down_grad_give")
    keep_down = down_grad(straight[:half], act, top, groups, "down_grad_keep")
    grad_w_down = scatter_pieces(lay, give_down, keep_down)

    grad_hidden, sum_up = hidden_back(tab, top, slope, down_pieces)

    size = width // groups
    if size % 128 == 0:
        order = tab

        def placed(a):
            return a
    else:
        order = straight

        def placed(a):
            return a.reshape(rows, groups, size)[:, tab].reshape(rows, width)

    def pair(a, g, name, places=None):
        a = placed(a)
        if size % 128 == 0:
            return (
                weight_grad(order[half:], a, g, groups, name + "_give", places),
                weight_grad(order[:half], a, g, groups, name + "_keep", places),
            )
        two = straight[:2]
        return (
            weight_grad(two[1:], a, g, 2, name + "_give", places),
            weight_grad(two[:1], a, g, 2, name + "_keep", places),
        )

    grad_w_up = scatter_pieces(lay, *pair(normed_two, grad_hidden[None], "up_grad", tab))
    grad_residual, branch, grad_mixed, sums_two = up_back(
        tab, grad_hidden, residual, top, gain_two, up_pieces, out_pieces
    )
    grad_w_out = scatter_pieces(lay, *pair(mixed, branch[None], "out_grad"))
    grads, sums_att = attention_back(tab, qkv, key_bias, grad_mixed, slots)
    grad_w_qkv = scatter_pieces(lay, *pair(normed_one, grads, "qkv_grad"))
    grad_patches, sums_one = qkv_back(
        tab, grads, x, grad_residual, gain_one, qkv_pieces, images, slots
    )

    eight_sums = jnp.stack(
        [
            sums_one[0],
            sums_one[1],
            sums_att[0],
            sums_att[2],
            sums_two[2],
            sums_two[0],
            sums_two[1],
            sums_two[3],
        ]
    )
    packed = jnp.concatenate(
        [
            eight_sums.reshape(8, ndev, own).transpose(1, 0, 2).reshape(ndev, 8 * own),
            sum_up.reshape(ndev, own_up),
        ],
        axis=1,
    )
    mine = scatter_small(lay, packed)[0]
    vecs = [mine[own * i : own * (i + 1)] for i in range(8)]
    return (
        block_out,
        grad_patches,
        vecs[0],
        vecs[1],
        grad_w_qkv,
        vecs[2],
        vecs[3],
        grad_w_out,
        vecs[4],
        vecs[5],
        vecs[6],
        grad_w_up,
        mine[8 * own :],
        grad_w_down,
        vecs[7],
    )


def solution(mesh):
    both = P(AXES)
    mat = P(AXES, None)
    cube = P(AXES, None, None)
    in_specs = (
        cube, mat, both, both, both, mat, both, both, mat, both, both, both, mat, both, mat, both,
        cube,
    )
    out_specs = (
        cube, cube, both, both, mat, both, both, mat, both, both, both, mat, both, mat, both,
    )
    return jax.shard_map(
        functools.partial(local, Layout(mesh)),
        mesh=mesh,
        in_specs=in_specs,
        out_specs=out_specs,
        check_vma=False,
    )
```

time: 1410 us -> 727 us (0.52)
  waiting for transfers between devices: 769 us -> 200 us
  Pallas kernels: 0 us -> 385 us
  matrix products: 289 us -> 0 us
  blocking collectives: 152 us -> 0 us
  local copies, waits for them, and re-layouts: 137 us -> 40.1 us
  starting transfers between devices: 0.32 us -> 59.7 us
    reduce_scatter x4 -> x0, waiting for transfers between devices: 764 us -> none  [the longest x1 365 us: local(): lax.psum_scatter(grad_w_down, ('wide', 'narrow'), scatter_dimension=0, ti...]
    pallas_call x0 -> x17, Pallas kernels: none -> 385 us  [the longest x1 100 us: attention_back(): call(body, (sds((3, rows, width), BF), sds((8, width), F32)), (pairs, row...]
    dot_general x18 -> x0, matrix products: 289 us -> none  [the longest x4 71.1 us: back_product(): lax.dot_general(left_side, right_side, (((1,), (1,)), ((), ())), preferre...]
    ppermute x0 -> x66, waiting for transfers between devices: none -> 200 us  [move(): return lax.ppermute(x, AXES, pairs)]
    unnamed x2 -> x0, blocking collectives: 85.5 us -> none
    all_gather x1 -> x0, blocking collectives: 66.8 us -> none  [local(): lax.all_gather(bias_up, ('wide', 'narrow'), axis=0, tiled=True)]
    reshape x11 -> x5, local copies, waits for them, and re-layouts: 67.2 us -> 4.77 us  [the longest x1 2.25 us: local(): x = patches.reshape(rows, width)]
    ppermute x0 -> x66, starting transfers between devices: none -> 59.7 us  [move(): return lax.ppermute(x, AXES, pairs)]
  transfers between devices with their start and end apart: 8 -> 66, of which waited for: 4 -> 26; matrix products, arithmetic and copies ran while one was open for 28% -> 9% of each run, Pallas kernels for 0% -> 45%
where the time goes in v1:
time: 727 us; the launch traced here: 722 us
  Pallas kernels  385 us (53%)
  waiting for transfers between devices  200 us (28%)
  starting transfers between devices  59.7 us (8%)
  local copies, waits for them, and re-layouts  40.1 us (6%)
  other arithmetic  35 us (5%)
    ppermute x66, waiting for transfers between devices, move(): return lax.ppermute(x, AXES, pairs)  200 us
    pallas_call x1, Pallas kernels, attention_back(): call(body, (sds((3, rows, width), BF), sds((8, width), F32)), (pairs, row...  100 us
    pallas_call x1, Pallas kernels, attention(): call(body, sds((rows, width), BF), (pairs, rows // blk), [pl.BlockSpec((b...  70.6 us
    ppermute x66, starting transfers between devices, move(): return lax.ppermute(x, AXES, pairs)  59.7 us
    pallas_call x6, Pallas kernels, weight_grad(): call(body, sds((count * size, parts * width), BF), (parts * per,), [pl.Bl...  54.7 us
    pallas_call x1, Pallas kernels, up_back(): call(body, (sds((rows, width), F32), sds((rows, width), BF), sds((rows, w...  32.9 us
    pallas_call x1, Pallas kernels, up_product(): call(body, (sds((rows, hid), BF), sds((rows, hid), BF)), (count,), [full(...  25 us
    pallas_call x2, Pallas kernels, down_grad(): call(body, sds((count * size, width), BF), (count,), [pl.BlockSpec((rows,...  20.3 us
  transfers between devices with their start and end apart: 66, of which 26 were waited for; matrix products, arithmetic and copies ran while one was open for 9% of the time, Pallas kernels for 45%

profile of v1, /device:TPU:0, one launch (start us, length us, event | category | flops | bytes accessed | tf_op | source)
XLA Modules:
  0.0 722.3 jit_solution(11097603465786959925)
XLA Ops:
  0.7 6.1 concatenate.102
  28.9 11.0 %collective-permute-done.23 = bf16[32,4096]{1,0:T(8,128)(2,1)S(1)} collective-permute-done((bf16[32,4096]{1,0:T(8,128)(2,1)}, bf16[32,4096]{1,0:T(8,128)(2,1)S(1)}, u32[]{:S(2)}, u32[]{:S(2)}) %collective-permute-start.23) | collective-permute-done | bytes 262176 | tf_op jit(solution)/shard_map/ppermute | solution.py:71
  46.7 18.2 %collective-permute-done.6 = bf16[64,3072]{1,0:T(8,128)(2,1)S(1)} collective-permute-done((bf16[64,3072]{1,0:T(8,128)(2,1)S(1)}, bf16[64,3072]{1,0:T(8,128)(2,1)S(1)}, u32[]{:S(2)}, u32[]{:S(2)}) %collective-permute-start.6) | collective-permute-done | bytes 393248 | tf_op jit(solution)/shard_map/ppermute | solution.py:71
  74.1 7.6 %collective-permute-done.24 = bf16[64,4096]{1,0:T(8,128)(2,1)S(1)} collective-permute-done((bf16[64,4096]{1,0:T(8,128)(2,1)S(1)}, bf16[64,4096]{1,0:T(8,128)(2,1)S(1)}, u32[]{:S(2)}, u32[]{:S(2)}) %collective-permute-start.24) | collective-permute-done | bytes 524320 | tf_op jit(solution)/shard_map/ppermute | solution.py:71
  86.2 6.0 collective-permute-done.33
  97.6 7.5 %collective-permute-done.8.rest_2_ = bf16[128,3072]{1,0:T(8,128)(2,1)S(1)} collective-permute-done((bf16[128,3072]{1,0:T(8,128)(2,1)S(1)}, bf16[128,3072]{1,0:T(8,128)(2,1)S(1)}, u32[]{:S(2)}, u32[]{:S(2)}) %collective-permute-start.8) | collective-permute-done | bytes 786464 | tf_op jit(solution)/shard_map/ppermute | solution.py:71
  132.0 16.3 %collective-permute-done.9.rest_3_ = bf16[128,3072]{1,0:T(8,128)(2,1)} collective-permute-done((bf16[128,3072]{1,0:T(8,128)(2,1)}, bf16[128,3072]{1,0:T(8,128)(2,1)}, u32[]{:S(2)}, u32[]{:S(2)}) %collective-permute-start.9) | collective-permute-done | bytes 786464 | tf_op jit(solution)/shard_map/ppermute | solution.py:71
  157.6 15.6 %qkv_product.1 = (bf16[1200,1024]{1,0:T(8,128)(2,1)}, bf16[1200,3072]{1,0:T(8,128)(2,1)}) custom-call(s32[8]{0:T(128)} %pad_add_fusion.tab_ref, bf16[1200,1024]{1,0:T(8,128)(2,1)} %reshape.118.x_ref, f32[1,1024]{1,0:T(1,128)} %unstack.49.g_ref, f32[1,1024]{1,0:T(1,128)} %unstack.51.b_ref, f32[1,3072]{1,0:T(1,128)} %pad_maximum_fusion.c_ref, ...), custom_call_target="tpu_custom_call" | custom-call | flops 7549747200 | bytes 18579456 | tf_op jit(solution)/shard_map/qkv_product/pallas_call | solution.py:244
  173.2 70.6 %attention.1.m_ref.rest_0_.rest_1_.rest_2_.rest_3_ = bf16[1200,1024]{1,0:T(8,128)(2,1)} custom-call(s32[8]{0:T(128)} %pad_add_fusion.tab_ref, bf16[1200,3072]{1,0:T(8,128)(2,1)} %get-tuple-element.31.q_ref.k_ref.v_ref, bf16[1200,3072]{1,0:T(8,128)(2,1)} %get-tuple-element.31.q_ref.k_ref.v_ref, bf16[1200,3072]{1,0:T(8,128)(2,1)} %get-tuple-element.31.q_ref.k_ref.v_ref, ...), custom_call_target="tpu_custom_call" | custom-call | flops 2516582400 | bytes 9830400 | tf_op jit(solution)/shard_map/attention/pallas_call | solution.py:309
  244.9 9.5 %out_product.1 = (f32[1200,1024]{1,0:T(8,128)}, bf16[1200,1024]{1,0:T(8,128)(2,1)}) custom-call(s32[8]{0:T(128)} %pad_add_fusion.tab_ref, bf16[1200,1024]{1,0:T(8,128)(2,1)} %attention.1.m_ref.rest_0_.rest_1_.rest_2_.rest_3_, bf16[1200,1024]{1,0:T(8,128)(2,1)} %reshape.118.x_ref, f32[1,1024]{1,0:T(1,128)} %unstack.57.c_ref, f32[1,1024]{1,0:T(1,128)} %unstack.59.g_ref, ...), custom_call_target="tpu_custom_call" | custom-call | flops 2516582400 | bytes 14385152 | tf_op jit(solution)/shard_map/out_product/pallas_call | solution.py:411
  254.5 25.0 %up_product.1 = (bf16[1200,4096]{1,0:T(8,128)(2,1)}, bf16[1200,4096]{1,0:T(8,128)(2,1)}) custom-call(s32[8]{0:T(128)} %pad_add_fusion.tab_ref, bf16[1200,1024]{1,0:T(8,128)(2,1)} %get-tuple-element.32.n_ref.rest_0_.rest_1_.rest_2_.rest_3_, f32[1,4096]{1,0:T(1,128)} %bitcast.38, bf16[128,4096]{1,0:T(8,128)(2,1)} %maximum_select_fusion.rest_0_, ...), custom_call_target="tpu_custom_call" | custom-call | flops 10213785600 | bytes 30507008 | tf_op jit(solution)/shard_map/up_product/pallas_call | solution.py:441
  279.5 18.9 %hidden_back.1 = (bf16[1200,4096]{1,0:T(8,128)(2,1)}, f32[1,4096]{1,0:T(1,128)}) custom-call(s32[8]{0:T(128)} %pad_add_fusion.tab_ref, bf16[1200,1024]{1,0:T(8,128)(2,1)} %broadcast_select_fusion.t_ref, bf16[1200,4096]{1,0:T(8,128)(2,1)} %get-tuple-element.35.d_ref, bf16[512,1024]{1,0:T(8,128)(2,1)} %maximum_select_fusion.1.rest_0_, ...), custom_call_target="tpu_custom_call" | custom-call | flops 10066329600 | bytes 30507008 | tf_op jit(solution)/shard_map/hidden_back/pallas_call | solution.py:525
  298.4 32.9 %up_back.1 = (f32[1200,1024]{1,0:T(8,128)}, bf16[1200,1024]{1,0:T(8,128)(2,1)}, bf16[1200,1024]{1,0:T(8,128)(2,1)}, f32[8,1024]{1,0:T(8,128)}) custom-call(s32[8]{0:T(128)} %pad_add_fusion.tab_ref, bf16[1200,4096]{1,0:T(8,128)(2,1)} %get-tuple-element.36.h_ref, f32[1200,1024]{1,0:T(8,128)} %get-tuple-element.34.r_ref, ...), custom_call_target="tpu_custom_call" | custom-call | flops 12582912000 | bytes 37879808 | tf_op jit(solution)/shard_map/up_back/pallas_call | solution.py:590
  332.9 10.2 %down_grad_give.1 = bf16[2048,1024]{1,0:T(8,128)(2,1)} custom-call(s32[4]{0:T(128)} %slice.181.tab_ref, bf16[1200,4096]{1,0:T(8,128)(2,1)} %get-tuple-element.33.a_ref, bf16[1200,1024]{1,0:T(8,128)(2,1)} %broadcast_select_fusion.t_ref), custom_call_target="tpu_custom_call" | custom-call | flops 5033164800 | bytes 11567104 | tf_op jit(solution)/shard_map/down_grad_give/pallas_call | solution.py:707
  343.5 12.6 %up_grad_give.1 = bf16[512,4096]{1,0:T(8,128)(2,1)} custom-call(s32[12]{0:T(128)} %get-tuple-element.128.tab_ref, bf16[1200,1024]{1,0:T(8,128)(2,1)} %get-tuple-element.32.n_ref.rest_0_.rest_1_.rest_2_.rest_3_, bf16[1200,1024]{1,0:T(8,128)(2,1)} %get-tuple-element.32.n_ref.rest_0_.rest_1_.rest_2_.rest_3_, ...), custom_call_target="tpu_custom_call" | custom-call | flops 5033164800 | bytes 15253504 | tf_op jit(solution)/shard_map/up_grad_give/pallas_call | solution.py:684
  356.2 5.4 out_grad_give.1
  362.0 100.2 %attention_back.1 = (bf16[3,1200,1024]{2,1,0:T(8,128)(2,1)}, f32[8,1024]{1,0:T(8,128)}) custom-call(s32[8]{0:T(128)} %pad_add_fusion.tab_ref, bf16[1200,3072]{1,0:T(8,128)(2,1)} %get-tuple-element.31.q_ref.k_ref.v_ref, bf16[1200,3072]{1,0:T(8,128)(2,1)} %get-tuple-element.31.q_ref.k_ref.v_ref, bf16[1200,3072]{1,0:T(8,128)(2,1)} %get-tuple-element.31.q_ref.k_ref.v_ref, ...), custom_call_target="tpu_custom_call" | custom-call | flops 6291456000 | bytes 17203200 | tf_op jit(solution)/shard_map/attention_back/pallas_call | solution.py:367
  462.2 9.6 %qkv_grad_give.1 = bf16[512,3072]{1,0:T(8,128)(2,1)} custom-call(s32[4]{0:T(128)} %copy-done.10, bf16[1200,1024]{1,0:T(8,128)(2,1)} %get-tuple-element.45.rest_0_.rest_1_.rest_2_.rest_3_, bf16[1200,1024]{1,0:T(8,128)(2,1)} %get-tuple-element.45.rest_0_.rest_1_.rest_2_.rest_3_, bf16[1200,1024]{1,0:T(8,128)(2,1)} %get-tuple-element.45.rest_0_.rest_1_.rest_2_.rest_3_, ...), custom_call_target="tpu_custom_call" | custom-call | flops 3774873600 | bytes 11747328 | tf_op jit(solution)/shard_map/qkv_grad_give/pallas_call | solution.py:684
  471.9 18.4 %qkv_back.1 = (bf16[24,50,1024]{2,1,0:T(8,128)(2,1)}, f32[8,1024]{1,0:T(8,128)}) custom-call(s32[8]{0:T(128)} %pad_add_fusion.tab_ref, bf16[3,1200,1024]{2,1,0:T(8,128)(2,1)} %get-tuple-element.38.d_ref.rest_4_, bf16[1200,1024]{1,0:T(8,128)(2,1)} %reshape.118.x_ref, f32[1200,1024]{1,0:T(8,128)} %get-tuple-element.39.r_ref, f32[1,1024]{1,0:T(1,128)} %unstack.49.g_ref, ...), custom_call_target="tpu_custom_call" | custom-call | flops 7549747200 | bytes 23494656 | tf_op jit(solution)/shard_map/qkv_back/pallas_call | solution.py:643
  493.2 19.2 %down_product.1 = bf16[24,50,1024]{2,1,0:T(8,128)(2,1)} custom-call(s32[8]{0:T(128)} %pad_add_fusion.tab_ref, bf16[1200,4096]{1,0:T(8,128)(2,1)} %get-tuple-element.33.a_ref, f32[1200,1024]{1,0:T(8,128)} %get-tuple-element.34.r_ref, f32[1,1024]{1,0:T(1,128)} %unstack.63.c_ref, f32[1200,1]{1,0:T(8,128)} %reshape.127.k_ref, ...), custom_call_target="tpu_custom_call" | custom-call | flops 10066329600 | bytes 25591808 | tf_op jit(solution)/shard_map/down_product/pallas_call | solution.py:481
  512.9 10.1 %down_grad_keep.1 = bf16[2048,1024]{1,0:T(8,128)(2,1)} custom-call(s32[4]{0:T(128)} %bitcast.39, bf16[1200,4096]{1,0:T(8,128)(2,1)} %get-tuple-element.33.a_ref, bf16[1200,1024]{1,0:T(8,128)(2,1)} %broadcast_select_fusion.t_ref), custom_call_target="tpu_custom_call" | custom-call | flops 5033164800 | bytes 11567104 | tf_op jit(solution)/shard_map/down_grad_keep/pallas_call | solution.py:707
  524.6 12.6 %up_grad_keep.1 = bf16[512,4096]{1,0:T(8,128)(2,1)} custom-call(s32[12]{0:T(128)} %get-tuple-element.127.tab_ref, bf16[1200,1024]{1,0:T(8,128)(2,1)} %get-tuple-element.32.n_ref.rest_0_.rest_1_.rest_2_.rest_3_, bf16[1200,1024]{1,0:T(8,128)(2,1)} %get-tuple-element.32.n_ref.rest_0_.rest_1_.rest_2_.rest_3_, ...), custom_call_target="tpu_custom_call" | custom-call | flops 5033164800 | bytes 15253504 | tf_op jit(solution)/shard_map/up_grad_keep/pallas_call | solution.py:684
  537.3 5.4 out_grad_keep.1
  546.3 9.3 %qkv_grad_keep.1 = bf16[512,3072]{1,0:T(8,128)(2,1)} custom-call(s32[4]{0:T(128)} %copy-done.9, bf16[1200,1024]{1,0:T(8,128)(2,1)} %get-tuple-element.45.rest_0_.rest_1_.rest_2_.rest_3_, bf16[1200,1024]{1,0:T(8,128)(2,1)} %get-tuple-element.45.rest_0_.rest_1_.rest_2_.rest_3_, bf16[1200,1024]{1,0:T(8,128)(2,1)} %get-tuple-element.45.rest_0_.rest_1_.rest_2_.rest_3_, ...), custom_call_target="tpu_custom_call" | custom-call | flops 3774873600 | bytes 11747328 | tf_op jit(solution)/shard_map/qkv_grad_keep/pallas_call | solution.py:684
  585.6 11.1 %collective-permute-done.47 = bf16[256,3072]{1,0:T(8,128)(2,1)S(1)} collective-permute-done((bf16[256,3072]{1,0:T(8,128)(2,1)S(1)}, bf16[256,3072]{1,0:T(8,128)(2,1)S(1)}, u32[]{:S(2)}, u32[]{:S(2)}) %collective-permute-start.47) | collective-permute-done | bytes 1572896 | tf_op jit(solution)/shard_map/ppermute | solution.py:71
  604.5 13.3 %collective-permute-done.48 = bf16[128,3072]{1,0:T(8,128)(2,1)S(1)} collective-permute-done((bf16[128,3072]{1,0:T(8,128)(2,1)S(1)}, bf16[128,3072]{1,0:T(8,128)(2,1)S(1)}, u32[]{:S(2)}, u32[]{:S(2)}) %collective-permute-start.48) | collective-permute-done | bytes 786464 | tf_op jit(solution)/shard_map/ppermute | solution.py:71
  620.9 6.7 collective-permute-done.57
  629.8 5.7 collective-permute-done.49
  635.6 25.7 %collective-permute-done.62 = bf16[1024,1024]{1,0:T(8,128)(2,1)S(1)} collective-permute-done((bf16[1024,1024]{1,0:T(8,128)(2,1)S(1)}, bf16[1024,1024]{1,0:T(8,128)(2,1)S(1)}, u32[]{:S(2)}, u32[]{:S(2)}) %collective-permute-start.62) | collective-permute-done | bytes 2097184 | tf_op jit(solution)/shard_map/ppermute | solution.py:71
  667.4 9.8 %collective-permute-done.63 = bf16[512,1024]{1,0:T(8,128)(2,1)S(1)} collective-permute-done((bf16[512,1024]{1,0:T(8,128)(2,1)S(1)}, bf16[512,1024]{1,0:T(8,128)(2,1)S(1)}, u32[]{:S(2)}, u32[]{:S(2)}) %collective-permute-start.63) | collective-permute-done | bytes 1048608 | tf_op jit(solution)/shard_map/ppermute | solution.py:71
  680.5 19.5 %collective-permute-done.59 = bf16[64,4096]{1,0:T(8,128)(2,1)S(1)} collective-permute-done((bf16[64,4096]{1,0:T(8,128)(2,1)S(1)}, bf16[64,4096]{1,0:T(8,128)(2,1)S(1)}, u32[]{:S(2)}, u32[]{:S(2)}) %collective-permute-start.59) | collective-permute-done | bytes 524320 | tf_op jit(solution)/shard_map/ppermute | solution.py:71
  700.2 9.8 %collective-permute-done.64 = bf16[256,1024]{1,0:T(8,128)(2,1)S(1)} collective-permute-done((bf16[256,1024]{1,0:T(8,128)(2,1)S(1)}, bf16[256,1024]{1,0:T(8,128)(2,1)S(1)}, u32[]{:S(2)}, u32[]{:S(2)}) %collective-permute-start.64) | collective-permute-done | bytes 524320 | tf_op jit(solution)/shard_map/ppermute | solution.py:71
  (275 shorter events, 160.6 us)
Async XLA Ops:
  20.2 24.8 %collective-permute-start.32 = (bf16[128,1024]{1,0:T(8,128)(2,1)}, bf16[128,1024]{1,0:T(8,128)(2,1)S(1)}, u32[]{:S(2)}, u32[]{:S(2)}) collective-permute-start(bf16[128,1024]{1,0:T(8,128)(2,1)} %param.33), channel_id=1, source_target_pairs={{0,1},{1,0},{2,3},{3,2},{4,5},{5,4},{6,7},{7,6},{8,9},{9,8},{10,11... | collective-permute-start | bytes 786440 | tf_op jit(solution)/shard_map/ppermute | solution.py:71
  23.3 23.4 %collective-permute-start.16 = (bf16[128,1024]{1,0:T(8,128)(2,1)S(1)}, bf16[128,1024]{1,0:T(8,128)(2,1)S(1)}, u32[]{:S(2)}, u32[]{:S(2)}) collective-permute-start(bf16[128,1024]{1,0:T(8,128)(2,1)S(1)} %maximum_select_fusion.6.rest_0_.rest_8_), channel_id=1, source_target_pairs={{0,8},{1,9},{2,10},{3,11},{4,20},{5,21},{6,22},{7,23},{8,0},{9,1},... | collective-permute-start | bytes 786440 | tf_op jit(solution)/shard_map/ppermute | solution.py:71
  27.8 37.1 %collective-permute-start.6 = (bf16[64,3072]{1,0:T(8,128)(2,1)S(1)}, bf16[64,3072]{1,0:T(8,128)(2,1)S(1)}, u32[]{:S(2)}, u32[]{:S(2)}) collective-permute-start(bf16[64,3072]{1,0:T(8,128)(2,1)S(1)} %maximum_select_fusion.5), channel_id=1, source_target_pairs={{0,2},{1,3},{2,0},{3,1},{4,6},{5,7},{6,4},{7,5},{8,10},{9,11},{10,... | collective-permute-start | bytes 1179656 | tf_op jit(solution)/shard_map/ppermute | solution.py:71
  41.1 40.7 %collective-permute-start.24 = (bf16[64,4096]{1,0:T(8,128)(2,1)S(1)}, bf16[64,4096]{1,0:T(8,128)(2,1)S(1)}, u32[]{:S(2)}, u32[]{:S(2)}) collective-permute-start(bf16[64,4096]{1,0:T(8,128)(2,1)S(1)} %maximum_select_fusion.3), channel_id=1, source_target_pairs={{0,2},{1,3},{2,0},{3,1},{4,6},{5,7},{6,4},{7,5},{8,10},{9,11},{10,... | collective-permute-start | bytes 1572872 | tf_op jit(solution)/shard_map/ppermute | solution.py:71
  41.3 25.3 %collective-permute-start.4 = (bf16[16,384]{1,0:T(8,128)(2,1)S(1)}, bf16[16,384]{1,0:T(8,128)(2,1)}, u32[]{:S(2)}, u32[]{:S(2)}) collective-permute-start(bf16[16,384]{1,0:T(8,128)(2,1)S(1)} %maximum_select_fusion.9), channel_id=1, source_target_pairs={{0,16},{1,17},{2,18},{3,19},{4,20},{5,21},{6,22},{7,23},{8,24},{9,... | collective-permute-start | bytes 36872 | tf_op jit(solution)/shard_map/ppermute | solution.py:71
  66.6 25.6 %collective-permute-start.33 = (bf16[256,1024]{1,0:T(8,128)(2,1)S(1)}, bf16[256,1024]{1,0:T(8,128)(2,1)S(1)}, u32[]{:S(2)}, u32[]{:S(2)}) collective-permute-start(bf16[256,1024]{1,0:T(8,128)(2,1)S(1)} %maximum_select_fusion.4), channel_id=1, source_target_pairs={{0,2},{1,3},{2,0},{3,1},{4,6},{5,7},{6,4},{7,5},{8,10},{9,11},{10,... | collective-permute-start | bytes 1572872 | tf_op jit(solution)/shard_map/ppermute | solution.py:71
  83.0 25.7 %collective-permute-start.25 = (bf16[128,4096]{1,0:T(8,128)(2,1)}, bf16[128,4096]{1,0:T(8,128)(2,1)}, u32[]{:S(2)}, u32[]{:S(2)}) collective-permute-start(bf16[128,4096]{1,0:T(8,128)(2,1)} %maximum_select_fusion.rest_0_), channel_id=1, source_target_pairs={{0,8},{1,9},{2,10},{3,11},{4,20},{5,21},{6,22},{7,23},{8,0},{9,1},... | collective-permute-start | bytes 3145736 | tf_op jit(solution)/shard_map/ppermute | solution.py:71
  92.2 35.1 %collective-permute-start.26 = (bf16[128,4096]{1,0:T(8,128)(2,1)}, bf16[128,4096]{1,0:T(8,128)(2,1)}, u32[]{:S(2)}, u32[]{:S(2)}) collective-permute-start(bf16[128,4096]{1,0:T(8,128)(2,1)} %maximum_select_fusion.rest_0_), channel_id=1, source_target_pairs={{0,16},{1,17},{2,18},{3,19},{4,12},{5,13},{6,14},{7,15},{8,24},{9,... | collective-permute-start | bytes 3145736 | tf_op jit(solution)/shard_map/ppermute | solution.py:71
  93.7 33.6 %collective-permute-start.28 = (bf16[128,4096]{1,0:T(8,128)(2,1)}, bf16[128,4096]{1,0:T(8,128)(2,1)}, u32[]{:S(2)}, u32[]{:S(2)}) collective-permute-start(bf16[128,4096]{1,0:T(8,128)(2,1)} %maximum_select_fusion.rest_0_), channel_id=1, source_target_pairs={{0,4},{1,5},{2,6},{3,7},{4,0},{5,1},{6,2},{7,3},{8,12},{9,13},{10,... | collective-permute-start | bytes 3145736 | tf_op jit(solution)/shard_map/ppermute | solution.py:71
  105.1 44.0 %collective-permute-start.34 = (bf16[512,1024]{1,0:T(8,128)(2,1)}, bf16[512,1024]{1,0:T(8,128)(2,1)}, u32[]{:S(2)}, u32[]{:S(2)}) collective-permute-start(bf16[512,1024]{1,0:T(8,128)(2,1)} %maximum_select_fusion.1.rest_0_), channel_id=1, source_target_pairs={{0,8},{1,9},{2,10},{3,11},{4,20},{5,21},{6,22},{7,23},{8,0},{9,1},... | collective-permute-start | bytes 3145736 | tf_op jit(solution)/shard_map/ppermute | solution.py:71
  108.8 42.3 %collective-permute-start.27 = (bf16[128,4096]{1,0:T(8,128)(2,1)}, bf16[128,4096]{1,0:T(8,128)(2,1)}, u32[]{:S(2)}, u32[]{:S(2)}) collective-permute-start(bf16[128,4096]{1,0:T(8,128)(2,1)} %collective-permute-done.25.rest_1_), channel_id=1, source_target_pairs={{0,16},{1,17},{2,18},{3,19},{4,12},{5,13},{6,14},{7,15},{8,24},{9,... | collective-permute-start | bytes 3145736 | tf_op jit(solution)/shard_map/ppermute | solution.py:71
  112.5 35.8 %collective-permute-start.9 = (bf16[128,3072]{1,0:T(8,128)(2,1)}, bf16[128,3072]{1,0:T(8,128)(2,1)}, u32[]{:S(2)}, u32[]{:S(2)}) collective-permute-start(bf16[128,3072]{1,0:T(8,128)(2,1)} %collective-permute-done.7.rest_1_), channel_id=1, source_target_pairs={{0,16},{1,17},{2,18},{3,19},{4,12},{5,13},{6,14},{7,15},{8,24},{9,... | collective-permute-start | bytes 2359304 | tf_op jit(solution)/shard_map/ppermute | solution.py:71
  149.1 94.7 %collective-permute-start.35 = (bf16[512,1024]{1,0:T(8,128)(2,1)}, bf16[512,1024]{1,0:T(8,128)(2,1)S(1)}, u32[]{:S(2)}, u32[]{:S(2)}) collective-permute-start(bf16[512,1024]{1,0:T(8,128)(2,1)} %maximum_select_fusion.1.rest_0_), channel_id=1, source_target_pairs={{0,16},{1,17},{2,18},{3,19},{4,12},{5,13},{6,14},{7,15},{8,24},{9,... | collective-permute-start | bytes 3145736 | tf_op jit(solution)/shard_map/ppermute | solution.py:71
  150.5 93.8 %collective-permute-start.29 = (bf16[128,4096]{1,0:T(8,128)(2,1)}, bf16[128,4096]{1,0:T(8,128)(2,1)}, u32[]{:S(2)}, u32[]{:S(2)}) collective-permute-start(bf16[128,4096]{1,0:T(8,128)(2,1)} %collective-permute-done.25.rest_1_), channel_id=1, source_target_pairs={{0,4},{1,5},{2,6},{3,7},{4,0},{5,1},{6,2},{7,3},{8,12},{9,13},{10,... | collective-permute-start | bytes 3145736 | tf_op jit(solution)/shard_map/ppermute | solution.py:71
  150.6 93.8 %collective-permute-start.30 = (bf16[128,4096]{1,0:T(8,128)(2,1)}, bf16[128,4096]{1,0:T(8,128)(2,1)}, u32[]{:S(2)}, u32[]{:S(2)}) collective-permute-start(bf16[128,4096]{1,0:T(8,128)(2,1)} %collective-permute-done.26.rest_2_), channel_id=1, source_target_pairs={{0,4},{1,5},{2,6},{3,7},{4,0},{5,1},{6,2},{7,3},{8,12},{9,13},{10,... | collective-permute-start | bytes 3145736 | tf_op jit(solution)/shard_map/ppermute | solution.py:71
  151.0 93.8 %collective-permute-start.36 = (bf16[512,1024]{1,0:T(8,128)(2,1)}, bf16[512,1024]{1,0:T(8,128)(2,1)}, u32[]{:S(2)}, u32[]{:S(2)}) collective-permute-start(bf16[512,1024]{1,0:T(8,128)(2,1)} %collective-permute-done.34.rest_1_), channel_id=1, source_target_pairs={{0,16},{1,17},{2,18},{3,19},{4,12},{5,13},{6,14},{7,15},{8,24},{9,... | collective-permute-start | bytes 3145736 | tf_op jit(solution)/shard_map/ppermute | solution.py:71
  157.4 97.0 %collective-permute-start.31 = (bf16[128,4096]{1,0:T(8,128)(2,1)}, bf16[128,4096]{1,0:T(8,128)(2,1)}, u32[]{:S(2)}, u32[]{:S(2)}) collective-permute-start(bf16[128,4096]{1,0:T(8,128)(2,1)} %collective-permute-done.27.rest_3_), channel_id=1, source_target_pairs={{0,4},{1,5},{2,6},{3,7},{4,0},{5,1},{6,2},{7,3},{8,12},{9,13},{10,... | collective-permute-start | bytes 3145736 | tf_op jit(solution)/shard_map/ppermute | solution.py:71
  243.8 35.6 %collective-permute-start.37 = (bf16[512,1024]{1,0:T(8,128)(2,1)}, bf16[512,1024]{1,0:T(8,128)(2,1)}, u32[]{:S(2)}, u32[]{:S(2)}) collective-permute-start(bf16[512,1024]{1,0:T(8,128)(2,1)} %maximum_select_fusion.1.rest_0_), channel_id=1, source_target_pairs={{0,4},{1,5},{2,6},{3,7},{4,0},{5,1},{6,2},{7,3},{8,12},{9,13},{10,... | collective-permute-start | bytes 3145736 | tf_op jit(solution)/shard_map/ppermute | solution.py:71
  244.3 35.2 %collective-permute-start.38 = (bf16[512,1024]{1,0:T(8,128)(2,1)}, bf16[512,1024]{1,0:T(8,128)(2,1)}, u32[]{:S(2)}, u32[]{:S(2)}) collective-permute-start(bf16[512,1024]{1,0:T(8,128)(2,1)} %collective-permute-done.34.rest_1_), channel_id=1, source_target_pairs={{0,4},{1,5},{2,6},{3,7},{4,0},{5,1},{6,2},{7,3},{8,12},{9,13},{10,... | collective-permute-start | bytes 3145736 | tf_op jit(solution)/shard_map/ppermute | solution.py:71
  244.4 35.1 %collective-permute-start.39 = (bf16[512,1024]{1,0:T(8,128)(2,1)S(1)}, bf16[512,1024]{1,0:T(8,128)(2,1)}, u32[]{:S(2)}, u32[]{:S(2)}) collective-permute-start(bf16[512,1024]{1,0:T(8,128)(2,1)S(1)} %collective-permute-done.35.rest_2_), channel_id=1, source_target_pairs={{0,4},{1,5},{2,6},{3,7},{4,0},{5,1},{6,2},{7,3},{8,12},{9,13},{10,... | collective-permute-start | bytes 3145736 | tf_op jit(solution)/shard_map/ppermute | solution.py:71
  244.8 34.7 %collective-permute-start.40 = (bf16[512,1024]{1,0:T(8,128)(2,1)}, bf16[512,1024]{1,0:T(8,128)(2,1)}, u32[]{:S(2)}, u32[]{:S(2)}) collective-permute-start(bf16[512,1024]{1,0:T(8,128)(2,1)} %collective-permute-done.36.rest_3_), channel_id=1, source_target_pairs={{0,4},{1,5},{2,6},{3,7},{4,0},{5,1},{6,2},{7,3},{8,12},{9,13},{10,... | collective-permute-start | bytes 3145736 | tf_op jit(solution)/shard_map/ppermute | solution.py:71
  343.1 256.0 %collective-permute-start.61 = (bf16[2048,1024]{1,0:T(8,128)(2,1)}, bf16[2048,1024]{1,0:T(8,128)(2,1)}, u32[]{:S(2)}, u32[]{:S(2)}) collective-permute-start(bf16[2048,1024]{1,0:T(8,128)(2,1)} %down_grad_give.1), channel_id=1, source_target_pairs={{0,4},{1,5},{2,6},{3,7},{4,0},{5,1},{6,2},{7,3},{8,12},{9,13},{10,... | collective-permute-start | bytes 12582920 | tf_op jit(solution)/shard_map/ppermute | solution.py:71
  356.1 224.2 %collective-permute-start.56 = (bf16[512,4096]{1,0:T(8,128)(2,1)}, bf16[512,4096]{1,0:T(8,128)(2,1)}, u32[]{:S(2)}, u32[]{:S(2)}) collective-permute-start(bf16[512,4096]{1,0:T(8,128)(2,1)} %up_grad_give.1), channel_id=1, source_target_pairs={{0,4},{1,5},{2,6},{3,7},{4,0},{5,1},{6,2},{7,3},{8,12},{9,13},{10,... | collective-permute-start | bytes 12582920 | tf_op jit(solution)/shard_map/ppermute | solution.py:71
  361.6 181.2 %collective-permute-start.51 = (bf16[512,1024]{1,0:T(8,128)(2,1)}, bf16[512,1024]{1,0:T(8,128)(2,1)}, u32[]{:S(2)}, u32[]{:S(2)}) collective-permute-start(bf16[512,1024]{1,0:T(8,128)(2,1)} %out_grad_give.1), channel_id=1, source_target_pairs={{0,4},{1,5},{2,6},{3,7},{4,0},{5,1},{6,2},{7,3},{8,12},{9,13},{10,... | collective-permute-start | bytes 3145736 | tf_op jit(solution)/shard_map/ppermute | solution.py:71
  471.8 101.2 %collective-permute-start.46 = (bf16[512,3072]{1,0:T(8,128)(2,1)}, bf16[512,3072]{1,0:T(8,128)(2,1)}, u32[]{:S(2)}, u32[]{:S(2)}) collective-permute-start(bf16[512,3072]{1,0:T(8,128)(2,1)} %qkv_grad_give.1), channel_id=1, source_target_pairs={{0,4},{1,5},{2,6},{3,7},{4,0},{5,1},{6,2},{7,3},{8,12},{9,13},{10,... | collective-permute-start | bytes 9437192 | tf_op jit(solution)/shard_map/ppermute | solution.py:71
  492.2 30.8 %collective-permute-start.41 = (f32[16,384]{1,0:T(8,128)S(1)}, f32[16,384]{1,0:T(8,128)S(1)}, u32[]{:S(2)}, u32[]{:S(2)}) collective-permute-start(f32[16,384]{1,0:T(8,128)S(1)} %fusion.2), channel_id=1, source_target_pairs={{0,16},{1,17},{2,18},{3,19},{4,20},{5,21},{6,22},{7,23},{8,24},{9,... | collective-permute-start | bytes 73736 | tf_op jit(solution)/shard_map/ppermute | solution.py:71
  584.3 43.3 %collective-permute-start.57 = (bf16[256,4096]{1,0:T(8,128)(2,1)S(1)}, bf16[256,4096]{1,0:T(8,128)(2,1)S(1)}, u32[]{:S(2)}, u32[]{:S(2)}) collective-permute-start(bf16[256,4096]{1,0:T(8,128)(2,1)S(1)} %slice.206), channel_id=1, source_target_pairs={{0,16},{1,17},{2,18},{3,19},{4,12},{5,13},{6,14},{7,15},{8,24},{9,... | collective-permute-start | bytes 6291464 | tf_op jit(solution)/shard_map/ppermute | solution.py:71
  603.6 57.7 %collective-permute-start.62 = (bf16[1024,1024]{1,0:T(8,128)(2,1)S(1)}, bf16[1024,1024]{1,0:T(8,128)(2,1)S(1)}, u32[]{:S(2)}, u32[]{:S(2)}) collective-permute-start(bf16[1024,1024]{1,0:T(8,128)(2,1)S(1)} %slice.211), channel_id=1, source_target_pairs={{0,16},{1,17},{2,18},{3,19},{4,12},{5,13},{6,14},{7,15},{8,24},{9,... | collective-permute-start | bytes 6291464 | tf_op jit(solution)/shard_map/ppermute | solution.py:71
  628.6 34.9 %collective-permute-start.58 = (bf16[128,4096]{1,0:T(8,128)(2,1)S(1)}, bf16[128,4096]{1,0:T(8,128)(2,1)S(1)}, u32[]{:S(2)}, u32[]{:S(2)}) collective-permute-start(bf16[128,4096]{1,0:T(8,128)(2,1)S(1)} %slice.208), channel_id=1, source_target_pairs={{0,8},{1,9},{2,10},{3,11},{4,20},{5,21},{6,22},{7,23},{8,0},{9,1},... | collective-permute-start | bytes 3145736 | tf_op jit(solution)/shard_map/ppermute | solution.py:71
  635.6 31.1 %collective-permute-start.50 = (bf16[32,3072]{1,0:T(8,128)(2,1)S(1)}, bf16[32,3072]{1,0:T(8,128)(2,1)S(1)}, u32[]{:S(2)}, u32[]{:S(2)}) collective-permute-start(bf16[32,3072]{1,0:T(8,128)(2,1)S(1)} %constant_dynamic-slice_fusion.6), channel_id=1, source_target_pairs={{0,1},{1,0},{2,3},{3,2},{4,5},{5,4},{6,7},{7,6},{8,9},{9,8},{10,11... | collective-permute-start | bytes 589832 | tf_op jit(solution)/shard_map/ppermute | solution.py:71
  663.8 36.2 %collective-permute-start.59 = (bf16[64,4096]{1,0:T(8,128)(2,1)S(1)}, bf16[64,4096]{1,0:T(8,128)(2,1)S(1)}, u32[]{:S(2)}, u32[]{:S(2)}) collective-permute-start(bf16[64,4096]{1,0:T(8,128)(2,1)S(1)} %constant_dynamic-slice_fusion.3), channel_id=1, source_target_pairs={{0,2},{1,3},{2,0},{3,1},{4,6},{5,7},{6,4},{7,5},{8,10},{9,11},{10,... | collective-permute-start | bytes 1572872 | tf_op jit(solution)/shard_map/ppermute | solution.py:71
  677.7 32.4 %collective-permute-start.64 = (bf16[256,1024]{1,0:T(8,128)(2,1)S(1)}, bf16[256,1024]{1,0:T(8,128)(2,1)S(1)}, u32[]{:S(2)}, u32[]{:S(2)}) collective-permute-start(bf16[256,1024]{1,0:T(8,128)(2,1)S(1)} %constant_dynamic-slice_fusion.1), channel_id=1, source_target_pairs={{0,2},{1,3},{2,0},{3,1},{4,6},{5,7},{6,4},{7,5},{8,10},{9,11},{10,... | collective-permute-start | bytes 1572872 | tf_op jit(solution)/shard_map/ppermute | solution.py:71
  (59 other events, 1096.3 us)
